TPU v7x, 32 devices: a whole 2x2x4 slice. The times are simulated.
32 devices in a mesh: ctx: 16 (over z, y, x), tp: 2 (over core).
Axes of the slice: x: 2, y: 2, z: 4, core: 2. Of those that a mesh axis runs over, the one named last changes fastest.
Arguments:
- query_in: bfloat16 [4096, 8192], P('ctx', 'tp'), may hold values from -6 to 6
- key_in: bfloat16 [4096, 8192], P('ctx', 'tp'), may hold values from -6 to 6
- value_in: bfloat16 [4096, 8192], P('ctx', 'tp'), may hold values from -6 to 6
- out_grad: bfloat16 [4096, 8192], P('ctx', 'tp'), may hold values from -400 to 400
- fill_counts: int32 [16], P('ctx'), may hold values from 192 to 256, as said below
- doc_starts: int32 [4], replicated, may hold values from 0 to 3071, as said below
- feat_taps: bfloat16 [3, 7, 8192], P(None, None, 'tp'), may hold values from -2 to 2
- mix_taps: bfloat16 [512, 128], P('tp'), may hold values from -0.5 to 0.5
- skip_gain: float32 [8192], P('tp'), may hold values from -4 to 4
Outputs:
- hyena_out: bfloat16 [4096, 8192], P('ctx', 'tp')
- query_grad: bfloat16 [4096, 8192], P('ctx', 'tp')
- key_grad: bfloat16 [4096, 8192], P('ctx', 'tp')
- value_grad: bfloat16 [4096, 8192], P('ctx', 'tp')
- mix_grad: float32 [512, 128], P('tp')
- skip_grad: float32 [8192], P('tp')
- feat_grad: float32 [3, 7, 8192], P(None, None, 'tp')
Inputs may be any that keep to these rules, and one draw needn't show every extreme that they name: `fill_counts`: entry s is the number of filled slots of shard s; the filled slots are a shard's first ones. Some shard is full. `doc_starts`: strictly increasing; the first entry is 0.
All inputs are finite; a program needn't handle non-finite values.
Results may differ from a plain program's by a relative error of at most 0.0075.
Values may be sent and summed in bfloat16 or wider, within the bound.
No kernel may reach another device: no remote copies, remote signals or barrier semaphores. Data moves between devices by JAX's collectives and lax.ppermute only.
A program may use at most 256 MiB of HBM per device.

v0:
```python
import math

import jax
import jax.numpy as jnp
from jax import lax
from jax.sharding import PartitionSpec as P


def prefix(value, axis, join, neutral):
    count, mine = (lax.axis_size(axis), lax.axis_index(axis))
    pieces = lax.all_gather(value, axis)
    so_far = jnp.full_like(value, 0) + jnp.asarray(neutral, value.dtype)

    def turn(position, so_far):
        longer = join(so_far, pieces[position])
        return jnp.where(position < mine, longer, so_far)

    return lax.fori_loop(0, count - 1, turn, so_far)


def from_behind(value, axis, steps):
    count = lax.axis_size(axis)
    leading, last = (max(0, -steps), min(count, count - steps))
    return lax.ppermute(value, axis, [(source, source + steps) for source in range(leading, last)])


def doc_index(positions, doc_starts):
    counted = jnp.sum((doc_starts[None, :] <= positions[:, None]).astype(jnp.int32), axis=1)
    return counted - 1


def banded(coeffs, block_rows):
    group_count, filter_len = coeffs.shape
    window = block_rows + filter_len - 1
    padded_row = jnp.concatenate(
        [coeffs, jnp.zeros((group_count, window + 1 - filter_len), coeffs.dtype)], axis=1
    )
    tiled = jnp.broadcast_to(padded_row[:, None, :], (group_count, block_rows, window + 1))
    tiled = tiled.reshape(group_count, block_rows * (window + 1))
    return tiled[:, : block_rows * window].reshape(group_count, block_rows, window)


def diagonals(products, filter_len):
    group_count, block_rows, window = products.shape
    flat = jnp.concatenate(
        [
            products.reshape(group_count, block_rows * window),
            jnp.zeros((group_count, block_rows), products.dtype),
        ],
        axis=1,
    )
    return jnp.sum(flat.reshape(group_count, block_rows, window + 1)[:, :, :filter_len], axis=1)


def contract(form, left, right):
    return jnp.einsum(form, left, right, preferred_element_type=jnp.float32)


def featurize(extended, doc_ext, weights):
    short_len = weights.shape[0]
    out_rows = extended.shape[0] - short_len + 1
    doc_out = doc_ext[short_len - 1 :]
    accum = jnp.zeros((out_rows, extended.shape[1]), jnp.float32)
    for j in range(short_len):
        offset = short_len - 1 - j
        source = extended[offset : offset + out_rows].astype(jnp.float32)
        same_doc = (doc_out == doc_ext[offset : offset + out_rows])[:, None]
        accum = accum + jnp.where(same_doc, weights[j].astype(jnp.float32) * source, 0.0)
    return accum


def unfeaturize(extended, doc_ext, weights):
    short_len = weights.shape[0]
    out_rows = extended.shape[0] - short_len + 1
    doc_out = doc_ext[:out_rows]
    accum = jnp.zeros((out_rows, extended.shape[1]), jnp.float32)
    for j in range(short_len):
        source = extended[j : j + out_rows].astype(jnp.float32)
        same_doc = (doc_out == doc_ext[j : j + out_rows])[:, None]
        accum = accum + jnp.where(same_doc, weights[j].astype(jnp.float32) * source, 0.0)
    return accum


def feat_grads(extended, doc_ext, grads):
    out_rows = grads.shape[0]
    short_len = extended.shape[0] - out_rows + 1
    doc_out = doc_ext[short_len - 1 :]
    pieces = []
    for j in range(short_len):
        offset = short_len - 1 - j
        source = extended[offset : offset + out_rows].astype(jnp.float32)
        same_doc = (doc_out == doc_ext[offset : offset + out_rows])[:, None]
        pieces.append(jnp.sum(jnp.where(same_doc, source * grads.astype(jnp.float32), 0.0), axis=0))
    return jnp.stack(pieces)


def mix_blocks(extended, doc_ext, band):
    group_count, block_rows, window = band.shape
    filter_len = window - block_rows + 1
    channels = extended.shape[1]
    per_group = channels // group_count
    out_rows = extended.shape[0] - filter_len + 1

    def mix_per_block(b):
        first = b * block_rows
        source = lax.dynamic_slice_in_dim(extended, first, window, 0).reshape(
            window, group_count, per_group
        )
        doc_src = lax.dynamic_slice_in_dim(doc_ext, first, window, 0)
        doc_out = doc_src[filter_len - 1 :]
        matrix = jnp.where(
            (doc_out[:, None] == doc_src[None, :])[None], band, jnp.zeros((), band.dtype)
        )
        return contract("gas,sgc->agc", matrix, source).reshape(block_rows, channels)

    blocks = lax.map(mix_per_block, jnp.arange(out_rows // block_rows, dtype=jnp.int32))
    return blocks.reshape(out_rows, channels)


def grad_blocks(ext_grad, doc_back, ext_mix, doc_long, row_grads, band):
    group_count, block_rows, window = band.shape
    filter_len = window - block_rows + 1
    out_rows, channels = row_grads.shape
    per_group = channels // group_count

    def grad_per_block(b):
        first = b * block_rows
        source = lax.dynamic_slice_in_dim(ext_grad, first, window, 0).reshape(
            window, group_count, per_group
        )
        doc_src = lax.dynamic_slice_in_dim(doc_back, first, window, 0)
        matrix = jnp.where(
            (doc_src[:block_rows, None] == doc_src[None, :])[None], band, jnp.zeros((), band.dtype)
        )
        back_rows = contract("gas,sgc->agc", matrix, source).reshape(block_rows, channels)
        mix_src = lax.dynamic_slice_in_dim(ext_mix, first, window, 0).reshape(
            window, group_count, per_group
        )
        doc_mix = lax.dynamic_slice_in_dim(doc_long, first, window, 0)
        own_rows = lax.dynamic_slice_in_dim(row_grads, first, block_rows, 0).reshape(
            block_rows, group_count, per_group
        )
        products = contract("agc,sgc->gas", own_rows, mix_src)
        products = jnp.where(
            (doc_mix[filter_len - 1 :, None] == doc_mix[None, :])[None], products, 0.0
        )
        return (back_rows, diagonals(products, filter_len))

    back_all, taps_all = lax.map(
        grad_per_block, jnp.arange(out_rows // block_rows, dtype=jnp.int32)
    )
    return (back_all.reshape(out_rows, channels), jnp.sum(taps_all, axis=0)[:, ::-1])


def add_counts(earlier, later_part):
    return earlier + later_part


def shards(
    query_in, key_in, value_in, out_grad, fill_counts, doc_starts, feat_taps, mix_taps, skip_gain
):
    row_count, channels = query_in.shape
    short_len = feat_taps.shape[1]
    group_count, filter_len = mix_taps.shape
    block_rows = math.gcd(row_count, 128)
    filled = fill_counts[0]
    offsets = prefix(fill_counts, "ctx", add_counts, jnp.zeros((1,), jnp.int32))
    first_pos = offsets[0]
    slot_pos = jnp.arange(row_count, dtype=jnp.int32)
    is_valid = (slot_pos < filled)[:, None]

    def tail_rows(source, count):
        return lax.dynamic_slice_in_dim(source, filled - count, count, 0)

    prev_short = from_behind(
        (
            tail_rows(query_in, short_len - 1),
            tail_rows(key_in, short_len - 1),
            tail_rows(value_in, short_len - 1),
        ),
        "ctx",
        1,
    )
    doc_short = doc_index(
        first_pos - short_len + 1 + jnp.arange(row_count + short_len - 1, dtype=jnp.int32),
        doc_starts,
    )
    ext_q = jnp.concatenate([prev_short[0], query_in], axis=0)
    ext_k = jnp.concatenate([prev_short[1], key_in], axis=0)
    ext_v = jnp.concatenate([prev_short[2], value_in], axis=0)
    query = featurize(ext_q, doc_short, feat_taps[0])
    keys = featurize(ext_k, doc_short, feat_taps[1])
    values = featurize(ext_v, doc_short, feat_taps[2])
    mix_in = (keys * values).astype(jnp.bfloat16)
    prev_mix = from_behind(tail_rows(mix_in, filter_len - 1), "ctx", 1)
    ext_mix = jnp.concatenate([prev_mix, mix_in], axis=0)
    doc_long = doc_index(
        first_pos - filter_len + 1 + jnp.arange(row_count + filter_len - 1, dtype=jnp.int32),
        doc_starts,
    )
    mixed = mix_blocks(ext_mix, doc_long, banded(mix_taps[:, ::-1], block_rows))
    gated = mixed + skip_gain[None, :] * mix_in.astype(jnp.float32)
    hyena_out = jnp.where(is_valid, query * gated, 0.0).astype(jnp.bfloat16)
    grad_f = out_grad.astype(jnp.float32)
    mix_grad_rows = jnp.where(is_valid, grad_f * query, 0.0).astype(jnp.bfloat16)
    query_back = jnp.where(is_valid, grad_f * gated, 0.0).astype(jnp.bfloat16)
    next_mix = from_behind(mix_grad_rows[: filter_len - 1], "ctx", -1)
    ext_grad = jnp.concatenate(
        [mix_grad_rows, jnp.zeros((filter_len - 1, channels), jnp.bfloat16)], axis=0
    )
    ext_grad = lax.dynamic_update_slice_in_dim(ext_grad, next_mix, filled, 0)
    doc_back = doc_index(
        first_pos + jnp.arange(row_count + filter_len - 1, dtype=jnp.int32), doc_starts
    )
    back_rows, taps_grad = grad_blocks(
        ext_grad, doc_back, ext_mix, doc_long, mix_grad_rows, banded(mix_taps, block_rows)
    )
    mix_back = back_rows + skip_gain[None, :] * mix_grad_rows.astype(jnp.float32)
    key_back = jnp.where(is_valid, mix_back * values, 0.0).astype(jnp.bfloat16)
    value_back = jnp.where(is_valid, mix_back * keys, 0.0).astype(jnp.bfloat16)
    next_grads = from_behind(
        (query_back[: short_len - 1], key_back[: short_len - 1], value_back[: short_len - 1]),
        "ctx",
        -1,
    )
    doc_near = doc_back[: row_count + short_len - 1]
    tail_pad = jnp.zeros((short_len - 1, channels), jnp.bfloat16)
    in_grads = []
    for which, back_part in enumerate((query_back, key_back, value_back)):
        extended = lax.dynamic_update_slice_in_dim(
            jnp.concatenate([back_part, tail_pad], axis=0), next_grads[which], filled, 0
        )
        in_grads.append(
            jnp.where(is_valid, unfeaturize(extended, doc_near, feat_taps[which]), 0.0).astype(
                jnp.bfloat16
            )
        )
    feat = jnp.stack(
        [
            feat_grads(ext_q, doc_short, query_back),
            feat_grads(ext_k, doc_short, key_back),
            feat_grads(ext_v, doc_short, value_back),
        ]
    )
    skip_part = jnp.sum(mix_in.astype(jnp.float32) * mix_grad_rows.astype(jnp.float32), axis=0)
    total_params = (group_count * filter_len + channels * (1 + 3 * short_len)) * lax.axis_size("tp")
    taps_sum, skip_sum, feat_sum = lax.psum((taps_grad, skip_part, feat), "ctx")
    local_sq = (
        jnp.sum(taps_sum * taps_sum) + jnp.sum(skip_sum * skip_sum) + jnp.sum(feat_sum * feat_sum)
    )
    whole_sq = lax.psum(local_sq, "tp")
    factor = lax.rsqrt(whole_sq / total_params + 1e-06)
    mix_out = taps_sum * factor
    skip_out = skip_sum * factor
    feat_out = feat_sum * factor
    return (hyena_out, in_grads[0], in_grads[1], in_grads[2], mix_out, skip_out, feat_out)


def solution(mesh):
    in_specs = (
        P("ctx", "tp"),
        P("ctx", "tp"),
        P("ctx", "tp"),
        P("ctx", "tp"),
        P("ctx"),
        P(),
        P(None, None, "tp"),
        P("tp", None),
        P("tp"),
    )
    out_specs = (
        P("ctx", "tp"),
        P("ctx", "tp"),
        P("ctx", "tp"),
        P("ctx", "tp"),
        P("tp", None),
        P("tp"),
        P(None, None, "tp"),
    )
    return jax.shard_map(shards, mesh=mesh, in_specs=in_specs, out_specs=out_specs, check_vma=False)
```

profile of v0, /device:TPU:0, one launch (start us, length us, event | category | flops | bytes accessed | tf_op | source)
XLA Modules:
  0.0 872.9 jit_solution(13265531830705147478)
XLA Ops:
  27.4 11.9 %all-reduce.7 = s32[16]{0:T(128)S(1)} all-reduce(s32[16]{0:T(128)S(1)} %dynamic-update-slice), channel_id=2, replica_groups=mesh['ctx'=16,'tp'=2] {'ctx'}, use_global_device_ids=true, to_apply=%add.7 | all-reduce | flops 16 | bytes 128
  39.3 18.9 %while.35 = (s32[]{:T(128)}, s32[1]{0:T(128)}, s32[]{:T(128)}, s32[16,1]{0,1:T(1,128)S(1)}, s32[]{:T(128)}) while((s32[]{:T(128)}, s32[1]{0:T(128)}, s32[]{:T(128)}, s32[16,1]{0,1:T(1,128)S(1)}, s32[]{:T(128)}) %tuple.135), condition=%wide.region_1.2_spmd, body=%wide.region_0.1_spmd.sunk | while | flops 5 | bytes 115 | solution.py:18
  59.2 30.3 %fusion.52 = (f32[4096]{0:T(1024)S(1)}, bf16[256,4096]{1,0:T(8,128)(2,1)S(1)}, bf16[256,4096]{1,0:T(8,128)(2,1)S(1)}, f32[256,4096]{1,0:T(8,128)}, f32[256,4096]{1,0:T(8,128)}, /*index=5*/f32[256,4096]{1,0:T(8,128)}) fusion(bf16[256,4096]{1,0:T(8,128)(2,1)} %param.18, pred[256]{0:T(512)(128)(4,1)S(1)} %iota_compare_fusion, bf16[256,4096]{1,0:T(8,128)(2,1)} %param.17, ...), kind=kLoop, calls=%fused_computation.127 | loop fusion | flops 148893696 | bytes 25675520 | tf_op jit(solution)/shard_map/reduce_sum | solution.py:245
  97.9 41.7 %copy.68 = bf16[32,8,128,256]{3,1,2,0:T(8,128)(2,1)S(1)} copy(bf16[32,8,128,256]{3,2,1,0:T(8,128)(2,1)S(1)} %bitcast.138) | data formatting | bytes 33554432
  146.2 56.8 %reshape.367 = bf16[256,128,255]{2,1,0:T(8,128)(2,1)} reshape(bf16[256,32640]{1,0:T(8,128)(2,1)} %slice.526) | data formatting | bytes 33423360 | tf_op jit(solution)/shard_map/reshape | solution.py:40
  204.2 41.7 %copy.67 = bf16[32,8,128,256]{3,1,2,0:T(8,128)(2,1)S(1)} copy(bf16[32,8,128,256]{3,2,1,0:T(8,128)(2,1)S(1)} %bitcast.139) | data formatting | bytes 33554432
  245.9 6.6 slice.516
  252.5 56.7 %reshape.364 = bf16[256,128,255]{2,1,0:T(8,128)(2,1)} reshape(bf16[256,32640]{1,0:T(8,128)(2,1)} %slice.516) | data formatting | bytes 33423360 | tf_op jit(solution)/shard_map/reshape | solution.py:40
  314.4 87.4 %psum.29 = f32[4096]{0:T(1024)S(1)} all-reduce(f32[4096]{0:T(1024)S(1)} %get-tuple-element.285), channel_id=1, replica_groups=mesh['ctx'=16,'tp'=2] {'ctx'}, use_global_device_ids=true, to_apply=%region_14.15 | all-reduce | flops 4096 | bytes 32768 | tf_op jit(solution)/shard_map/psum | solution.py:247
  410.1 38.5 %while.36 = (s32[]{:T(128)}, f32[2,128,4096]{2,1,0:T(8,128)}, s32[2]{0:T(128)S(1)}, bf16[383,4096]{0,1:T(8,128)(2,1)}, s32[383]{0:T(512)S(1)}, /*index=5*/bf16[2...) while((s32[]{:T(128)}, f32[2,128,4096]{2,1,0:T(8,128)}, s32[2]{0:T(128)S(1)}, ...), condition=%wide.region_5.6_spmd, body=%wide.region_4.5_spmd.sunk | while | flops 275775360 | bytes 33534376 | solution.py:116
  414.6 11.5 %fusion.126 = f32[256,16,128]{2,1,0:T(8,128)} fusion(bf16[255,256,16]{0,2,1:T(8,128)(2,1)S(1)} %bitcast.142, bf16[256,128,255]{2,1,0:T(8,128)(2,1)} %get-tuple-element.492, pred[128,255]{1,0:T(8,128)(4,1)S(1)} %broadcast_compare_fusion.6), kind=kOutput, calls=%fused_computation.1.clone.1 | convolution fusion | flops 275742720 | bytes 20930432 | tf_op jit(solution)/shard_map/while/body/eval_jaxpr/gas,sgc->agc/dot_general | solution.py:56
  433.7 11.5 %fusion.126 = f32[256,16,128]{2,1,0:T(8,128)} fusion(bf16[255,256,16]{0,2,1:T(8,128)(2,1)S(1)} %bitcast.142, bf16[256,128,255]{2,1,0:T(8,128)(2,1)} %get-tuple-element.492, pred[128,255]{1,0:T(8,128)(4,1)S(1)} %broadcast_compare_fusion.6), kind=kOutput, calls=%fused_computation.1.clone.1 | convolution fusion | flops 275742720 | bytes 20930432 | tf_op jit(solution)/shard_map/while/body/eval_jaxpr/gas,sgc->agc/dot_general | solution.py:56
  448.6 16.1 %fusion.65 = (f32[4096]{0:T(1024)}, f32[4096]{0:T(1024)}, f32[4096]{0:T(1024)}, f32[4096]{0:T(1024)}, f32[4096]{0:T(1024)}, /*index=5*/f32[4096]{0:T(1024)}, bf16[256,4096]{1,0:T(8,128)(2,1)S(1)}) fusion(bf16[256,4096]{1,0:T(8,128)(2,1)} %param.15, bf16[6,4096]{1,0:T(8,128)(2,1)S(1)} %collective-permute-done, pred[256]{0:T(512)(128)(4,1)S(1)} %get-tuple-element.326, ...), kind=kLoop, calls=%fused_computation.140 | loop fusion | flops 52404224 | bytes 12748544 | tf_op jit(solution)/shard_map/reduce_sum | solution.py:93
  468.3 6.6 dynamic_update_slice.24
  477.4 216.3 %while.37 = (s32[]{:T(128)}, f32[2,128,4096]{2,1,0:T(8,128)}, f32[2,256,128]{2,1,0:T(8,128)S(1)}, s32[2]{0:T(128)S(1)}, bf16[383,4096]{1,0:T(8,128)(2,1)}, /*ind...) while((s32[]{:T(128)}, f32[2,128,4096]{2,1,0:T(8,128)}, ...), condition=%wide.region_9.10_spmd, body=%wide.region_7.9_spmd.sunk | while | flops 555712256 | bytes 330138688 | solution.py:149
  487.6 12.2 %fusion.131 = f32[256,16,128]{2,1,0:T(8,128)} fusion(bf16[255,256,16]{0,2,1:T(8,128)(2,1)} %bitcast.144, bf16[256,128,255]{2,1,0:T(8,128)(2,1)} %get-tuple-element.535, pred[128,255]{1,0:T(8,128)(4,1)S(1)} %broadcast_compare_fusion.7), kind=kOutput, calls=%fused_computation.11.clone.1 | convolution fusion | flops 275742720 | bytes 20930432 | tf_op jit(solution)/shard_map/while/body/eval_jaxpr/gas,sgc->agc/dot_general | solution.py:56
  504.0 13.1 %broadcast_select_fusion.2 = f32[256,128,255]{2,1,0:T(8,128)} fusion(pred[128,255]{1,0:T(8,128)(4,1)S(1)} %broadcast_compare_fusion.8, bf16[128,256,16]{0,2,1:T(8,128)(2,1)S(1)} %bitcast.137, bf16[255,256,16]{0,2,1:T(8,128)(2,1)S(1)} %bitcast.136), kind=kOutput, calls=%fused_computation.10.clone.1 | convolution fusion | flops 275742720 | bytes 36593536 | tf_op jit(solution)/shard_map/while/body/eval_jaxpr/agc,sgc->gas/dot_general | solution.py:56
  517.1 33.4 %reshape.397 = f32[256,32640]{1,0:T(8,128)} reshape(f32[256,128,255]{2,1,0:T(8,128)} %broadcast_select_fusion.2) | data formatting | bytes 66846720 | tf_op jit(solution)/shard_map/while/body/eval_jaxpr/reshape | solution.py:47
  550.6 11.9 %concatenate.44 = f32[256,32768]{1,0:T(8,128)S(1)} pad(f32[256,32640]{1,0:T(8,128)} %reshape.397, f32[]{:T(128)} %constant.103.clone.1..sunk), padding=0_0x0_128 | pad | bytes 66977796 | tf_op jit(solution)/shard_map/while/body/eval_jaxpr/concatenate | solution.py:45
  562.5 14.5 %copy.78 = f32[32,8,128,256]{3,2,1,0:T(8,128)} copy(f32[32,8,128,256]{3,1,2,0:T(8,128)S(1)} %bitcast.134) | data formatting | bytes 67108864 | tf_op jit(solution)/shard_map/while
  577.0 8.5 slice_reduce_fusion.2
  595.2 12.2 %fusion.131 = f32[256,16,128]{2,1,0:T(8,128)} fusion(bf16[255,256,16]{0,2,1:T(8,128)(2,1)} %bitcast.144, bf16[256,128,255]{2,1,0:T(8,128)(2,1)} %get-tuple-element.535, pred[128,255]{1,0:T(8,128)(4,1)S(1)} %broadcast_compare_fusion.7), kind=kOutput, calls=%fused_computation.11.clone.1 | convolution fusion | flops 275742720 | bytes 20930432 | tf_op jit(solution)/shard_map/while/body/eval_jaxpr/gas,sgc->agc/dot_general | solution.py:56
  611.7 13.1 %broadcast_select_fusion.2 = f32[256,128,255]{2,1,0:T(8,128)} fusion(pred[128,255]{1,0:T(8,128)(4,1)S(1)} %broadcast_compare_fusion.8, bf16[128,256,16]{0,2,1:T(8,128)(2,1)S(1)} %bitcast.137, bf16[255,256,16]{0,2,1:T(8,128)(2,1)S(1)} %bitcast.136), kind=kOutput, calls=%fused_computation.10.clone.1 | convolution fusion | flops 275742720 | bytes 36593536 | tf_op jit(solution)/shard_map/while/body/eval_jaxpr/agc,sgc->gas/dot_general | solution.py:56
  624.8 33.4 %reshape.397 = f32[256,32640]{1,0:T(8,128)} reshape(f32[256,128,255]{2,1,0:T(8,128)} %broadcast_select_fusion.2) | data formatting | bytes 66846720 | tf_op jit(solution)/shard_map/while/body/eval_jaxpr/reshape | solution.py:47
  658.3 11.9 %concatenate.44 = f32[256,32768]{1,0:T(8,128)S(1)} pad(f32[256,32640]{1,0:T(8,128)} %reshape.397, f32[]{:T(128)} %constant.103.clone.1..sunk), padding=0_0x0_128 | pad | bytes 66977796 | tf_op jit(solution)/shard_map/while/body/eval_jaxpr/concatenate | solution.py:45
  670.1 14.5 %copy.78 = f32[32,8,128,256]{3,2,1,0:T(8,128)} copy(f32[32,8,128,256]{3,1,2,0:T(8,128)S(1)} %bitcast.134) | data formatting | bytes 67108864 | tf_op jit(solution)/shard_map/while
  684.6 8.5 slice_reduce_fusion.2
  693.7 16.8 %fusion.78 = (f32[4096]{0:T(1024)}, f32[4096]{0:T(1024)}, f32[4096]{0:T(1024)}, f32[4096]{0:T(1024)}, f32[4096]{0:T(1024)}, /*index=5*/f32[4096]{0:T(1024)}, bf16[256,4096]{1,0:T(8,128)(2,1)S(1)}) fusion(bf16[256,4096]{1,0:T(8,128)(2,1)} %param.16, bf16[6,4096]{1,0:T(8,128)(2,1)S(1)} %copy-done.21, pred[256]{0:T(512)(128)(4,1)} %copy-done.107, ...), kind=kLoop, calls=%fused_computation.153 | loop fusion | flops 51355648 | bytes 14845696 | tf_op jit(solution)/shard_map/reduce_sum | solution.py:93
  714.2 8.4 fusion.91
  737.0 7.3 select_convert_fusion.4
  746.1 14.5 %select_convert_fusion = bf16[256,4096]{1,0:T(8,128)(2,1)} fusion(bf16[262,4096]{1,0:T(8,128)(2,1)} %dynamic_update_slice.26, f32[4096]{0:T(1024)S(1)} %bitcast.190, f32[4096]{0:T(1024)S(1)} %bitcast.188, f32[4096]{0:T(1024)S(1)} %bitcast.164, f32[4096]{0:T(1024)S(1)} %bitcast.166, f32[4096]{0:T(1024)S(1)} %bitcast.168, f32[4096]{0:T(1024)S(1)} %bitcast.170, ...), kind=kLoop, calls=%fused_computation.167 | loop fusion | flops 29360128 | bytes 16893696 | tf_op jit(solution)/shard_map/convert_element_type | solution.py:234
  761.1 87.1 %all-reduce.11.cloned.1.call-done = (f32[256,128]{1,0:T(8,128)}, f32[3,7,4096]{2,1,0:T(8,128)}) async-done(((f32[256,128]{1,0:T(8,128)}, f32[3,7,4096]{2,1,0:T(8,128)}), (f32[256,128]{1,0:T(8,128)}, f32[3,7,4096]{2,1,0:T(8,128)})) %all-reduce.11.cloned.1.call-update) | async-done | bytes 475152 | tf_op jit(solution)/shard_map/psum | solution.py:247
  (392 shorter events, 139.2 us)
Async XLA Ops:
  7.2 841.1 %all-reduce.11.cloned.1.call-start = ((), (), s32[]{:S(2)}) async-start(), calls=%async_computation | async-start | bytes 1048576 | tf_op jit(solution)/shard_map/psum | solution.py:247
  8.8 50.4 %collective-permute-start.2 = (bf16[6,4096]{1,0:T(8,128)(2,1)S(1)}, bf16[6,4096]{1,0:T(8,128)(2,1)S(1)}, u32[]{:S(2)}, u32[]{:S(2)}) collective-permute-start(bf16[6,4096]{1,0:T(8,128)(2,1)S(1)} %constant_dynamic-slice_fusion.6), channel_id=1, source_target_pairs={{0,2},{2,4},{4,6},{6,8},{8,10},{10,12},{12,14},{14,16},{16,18},{18... | collective-permute-start | bytes 147464 | tf_op jit(solution)/shard_map/ppermute | solution.py:24
  14.6 44.6 %collective-permute-start.1 = (bf16[6,4096]{1,0:T(8,128)(2,1)S(1)}, bf16[6,4096]{1,0:T(8,128)(2,1)S(1)}, u32[]{:S(2)}, u32[]{:S(2)}) collective-permute-start(bf16[6,4096]{1,0:T(8,128)(2,1)S(1)} %constant_dynamic-slice_fusion.7), channel_id=1, source_target_pairs={{0,2},{2,4},{4,6},{6,8},{8,10},{10,12},{12,14},{14,16},{16,18},{18... | collective-permute-start | bytes 147464 | tf_op jit(solution)/shard_map/ppermute | solution.py:24
  19.0 40.3 %collective-permute-start = (bf16[6,4096]{1,0:T(8,128)(2,1)S(1)}, bf16[6,4096]{1,0:T(8,128)(2,1)S(1)}, u32[]{:S(2)}, u32[]{:S(2)}) collective-permute-start(bf16[6,4096]{1,0:T(8,128)(2,1)S(1)} %constant_dynamic-slice_fusion.8), channel_id=1, source_target_pairs={{0,2},{2,4},{4,6},{6,8},{8,10},{10,12},{12,14},{14,16},{16,18},{18... | collective-permute-start | bytes 147464 | tf_op jit(solution)/shard_map/ppermute | solution.py:24
  23.3 66.3 %copy-start.64 = (f32[1,1,4096]{2,1,0:T(1,128)}, f32[1,1,4096]{2,1,0:T(1,128)S(1)}, u32[]{:S(2)}) copy-start(f32[1,1,4096]{2,1,0:T(1,128)S(1)} %get-tuple-element.313) | copy-start | bytes 49156
  23.3 66.3 %copy-start.66 = (f32[1,1,4096]{2,1,0:T(1,128)}, f32[1,1,4096]{2,1,0:T(1,128)S(1)}, u32[]{:S(2)}) copy-start(f32[1,1,4096]{2,1,0:T(1,128)S(1)} %get-tuple-element.314) | copy-start | bytes 49156
  25.2 64.4 %copy-start.26 = (f32[1,1,4096]{2,1,0:T(1,128)}, f32[1,1,4096]{2,1,0:T(1,128)S(1)}, u32[]{:S(2)}) copy-start(f32[1,1,4096]{2,1,0:T(1,128)S(1)} %get-tuple-element.300) | copy-start | bytes 49156
  25.2 64.4 %copy-start.28 = (f32[1,1,4096]{2,1,0:T(1,128)}, f32[1,1,4096]{2,1,0:T(1,128)S(1)}, u32[]{:S(2)}) copy-start(f32[1,1,4096]{2,1,0:T(1,128)S(1)} %get-tuple-element.301) | copy-start | bytes 49156
  25.2 64.4 %copy-start.30 = (f32[1,1,4096]{2,1,0:T(1,128)}, f32[1,1,4096]{2,1,0:T(1,128)S(1)}, u32[]{:S(2)}) copy-start(f32[1,1,4096]{2,1,0:T(1,128)S(1)} %get-tuple-element.302) | copy-start | bytes 49156
  25.2 64.4 %copy-start.32 = (f32[1,1,4096]{2,1,0:T(1,128)}, f32[1,1,4096]{2,1,0:T(1,128)S(1)}, u32[]{:S(2)}) copy-start(f32[1,1,4096]{2,1,0:T(1,128)S(1)} %get-tuple-element.303) | copy-start | bytes 49156
  59.1 389.5 %copy-start.97 = (pred[256]{0:T(512)(128)(4,1)}, pred[256]{0:T(512)(128)(4,1)S(1)}, u32[]{:S(2)}) copy-start(pred[256]{0:T(512)(128)(4,1)S(1)} %get-tuple-element.321) | copy-start | bytes 772
  59.1 389.5 %copy-start.99 = (pred[256]{0:T(512)(128)(4,1)}, pred[256]{0:T(512)(128)(4,1)S(1)}, u32[]{:S(2)}) copy-start(pred[256]{0:T(512)(128)(4,1)S(1)} %get-tuple-element.322) | copy-start | bytes 772
  59.1 389.5 %copy-start.101 = (pred[256]{0:T(512)(128)(4,1)}, pred[256]{0:T(512)(128)(4,1)S(1)}, u32[]{:S(2)}) copy-start(pred[256]{0:T(512)(128)(4,1)S(1)} %get-tuple-element.323) | copy-start | bytes 772
  59.1 389.5 %copy-start.103 = (pred[256]{0:T(512)(128)(4,1)}, pred[256]{0:T(512)(128)(4,1)S(1)}, u32[]{:S(2)}) copy-start(pred[256]{0:T(512)(128)(4,1)S(1)} %get-tuple-element.324) | copy-start | bytes 772
  59.1 389.5 %copy-start.105 = (pred[256]{0:T(512)(128)(4,1)}, pred[256]{0:T(512)(128)(4,1)S(1)}, u32[]{:S(2)}) copy-start(pred[256]{0:T(512)(128)(4,1)S(1)} %get-tuple-element.325) | copy-start | bytes 772
  59.1 389.5 %copy-start.107 = (pred[256]{0:T(512)(128)(4,1)}, pred[256]{0:T(512)(128)(4,1)S(1)}, u32[]{:S(2)}) copy-start(pred[256]{0:T(512)(128)(4,1)S(1)} %get-tuple-element.326) | copy-start | bytes 772
  59.2 389.5 %copy-start.94 = (pred[256]{0:T(512)(128)(4,1)}, pred[256]{0:T(512)(128)(4,1)S(1)}, u32[]{:S(2)}) copy-start(pred[256]{0:T(512)(128)(4,1)S(1)} %iota_compare_fusion) | copy-start | bytes 772
  89.8 221.3 %copy-start.3 = (bf16[256,4096]{1,0:T(8,128)(2,1)}, bf16[256,4096]{1,0:T(8,128)(2,1)S(1)}, u32[]{:S(2)}) copy-start(bf16[256,4096]{1,0:T(8,128)(2,1)S(1)} %get-tuple-element.505) | copy-start | bytes 6291460
  91.4 311.1 %collective-permute-start.3 = (bf16[127,4096]{1,0:T(8,128)(2,1)S(1)}, bf16[127,4096]{1,0:T(8,128)(2,1)}, u32[]{:S(2)}, u32[]{:S(2)}) collective-permute-start(bf16[127,4096]{1,0:T(8,128)(2,1)S(1)} %constant_dynamic-slice_fusion.5), channel_id=1, source_target_pairs={{0,2},{2,4},{4,6},{6,8},{8,10},{10,12},{12,14},{14,16},{16,18},{18... | collective-permute-start | bytes 3121160 | tf_op jit(solution)/shard_map/ppermute | solution.py:24
  313.1 155.2 %collective-permute-start.5 = (bf16[127,4096]{1,0:T(8,128)(2,1)}, bf16[127,4096]{1,0:T(8,128)(2,1)}, u32[]{:S(2)}, u32[]{:S(2)}) collective-permute-start(bf16[127,4096]{1,0:T(8,128)(2,1)} %slice.525), channel_id=1, source_target_pairs={{2,0},{4,2},{6,4},{8,6},{10,8},{12,10},{14,12},{16,14},{18,16},{20... | collective-permute-start | bytes 3121160 | tf_op jit(solution)/shard_map/ppermute | solution.py:24
  477.4 216.3 %copy-start.21 = (bf16[6,4096]{1,0:T(8,128)(2,1)S(1)}, bf16[6,4096]{1,0:T(8,128)(2,1)}, u32[]{:S(2)}) copy-start(bf16[6,4096]{1,0:T(8,128)(2,1)} %copy-done.20) | copy-start | bytes 147460
  477.4 216.3 %copy-start.25 = (f32[4096]{0:T(1024)S(1)}, f32[4096]{0:T(1024)}, u32[]{:S(2)}) copy-start(f32[4096]{0:T(1024)} %param.23) | copy-start | bytes 49156
  729.0 7.0 collective-permute-start.4
  731.2 13.1 %collective-permute-start.7 = (bf16[6,4096]{1,0:T(8,128)(2,1)S(1)}, bf16[6,4096]{1,0:T(8,128)(2,1)S(1)}, u32[]{:S(2)}, u32[]{:S(2)}) collective-permute-start(bf16[6,4096]{1,0:T(8,128)(2,1)S(1)} %slice.535), channel_id=1, source_target_pairs={{2,0},{4,2},{6,4},{8,6},{10,8},{12,10},{14,12},{16,14},{18,16},{20... | collective-permute-start | bytes 147464 | tf_op jit(solution)/shard_map/ppermute | solution.py:24
  732.5 28.1 %collective-permute-start.6 = (bf16[6,4096]{1,0:T(8,128)(2,1)S(1)}, bf16[6,4096]{1,0:T(8,128)(2,1)S(1)}, u32[]{:S(2)}, u32[]{:S(2)}) collective-permute-start(bf16[6,4096]{1,0:T(8,128)(2,1)S(1)} %copy-done.82), channel_id=1, source_target_pairs={{2,0},{4,2},{6,4},{8,6},{10,8},{12,10},{14,12},{16,14},{18,16},{20... | collective-permute-start | bytes 147464 | tf_op jit(solution)/shard_map/ppermute | solution.py:24
  746.0 107.5 %copy-start.27 = (f32[1,1,4096]{2,1,0:T(1,128)S(1)}, f32[1,1,4096]{2,1,0:T(1,128)}, u32[]{:S(2)}) copy-start(f32[1,1,4096]{2,1,0:T(1,128)} %copy-done.26) | copy-start | bytes 49156
  746.0 107.5 %copy-start.29 = (f32[1,1,4096]{2,1,0:T(1,128)S(1)}, f32[1,1,4096]{2,1,0:T(1,128)}, u32[]{:S(2)}) copy-start(f32[1,1,4096]{2,1,0:T(1,128)} %copy-done.28) | copy-start | bytes 49156
  746.0 107.5 %copy-start.31 = (f32[1,1,4096]{2,1,0:T(1,128)S(1)}, f32[1,1,4096]{2,1,0:T(1,128)}, u32[]{:S(2)}) copy-start(f32[1,1,4096]{2,1,0:T(1,128)} %copy-done.30) | copy-start | bytes 49156
  746.0 107.5 %copy-start.33 = (f32[1,1,4096]{2,1,0:T(1,128)S(1)}, f32[1,1,4096]{2,1,0:T(1,128)}, u32[]{:S(2)}) copy-start(f32[1,1,4096]{2,1,0:T(1,128)} %copy-done.32) | copy-start | bytes 49156
  746.0 107.5 %copy-start.35 = (f32[1,1,4096]{2,1,0:T(1,128)S(1)}, f32[1,1,4096]{2,1,0:T(1,128)}, u32[]{:S(2)}) copy-start(f32[1,1,4096]{2,1,0:T(1,128)} %copy-done.34) | copy-start | bytes 49156
  746.1 107.5 %copy-start.37 = (f32[1,1,4096]{2,1,0:T(1,128)S(1)}, f32[1,1,4096]{2,1,0:T(1,128)}, u32[]{:S(2)}) copy-start(f32[1,1,4096]{2,1,0:T(1,128)} %copy-done.36) | copy-start | bytes 49156
  746.1 107.5 %copy-start.39 = (f32[1,1,4096]{2,1,0:T(1,128)S(1)}, f32[1,1,4096]{2,1,0:T(1,128)}, u32[]{:S(2)}) copy-start(f32[1,1,4096]{2,1,0:T(1,128)} %copy-done.38) | copy-start | bytes 49156
  (104 other events, 1771.2 us)
Sparse Core Ops, SparseCore 0:
  736.1 112.0 all-reduce.10
where the time goes:
time: 879 us; the launch traced here: 873 us
  local copies, waits for them, and re-layouts  418 us (48%)
  other arithmetic  137 us (16%)
  blocking collectives  102 us (12%)
  waiting for transfers between devices  87.1 us (10%)
  matrix products  73.7 us (8%)
  starting transfers between devices  21.7 us (2%)
  between operations  19.3 us (2%)
  loops' own time  13.8 us (2%)
    reshape x2, local copies, waits for them, and re-layouts, banded(): tiled[:, :block_rows * window].reshape(group_count, block_rows, window)  114 us
    unnamed x223, local copies, waits for them, and re-layouts  89.1 us
    psum x1, blocking collectives, shards(): taps_sum, skip_sum, feat_sum = lax.psum((taps_grad, skip_part, feat), 'ctx')  87.4 us
    psum x1, waiting for transfers between devices, shards(): taps_sum, skip_sum, feat_sum = lax.psum((taps_grad, skip_part, feat), 'ctx')  87.1 us
    dot_general x6, matrix products, contract(): return jnp.einsum(form, left, right, preferred_element_type=jnp.float32)  73.7 us
    reshape x2, local copies, waits for them, and re-layouts, diagonals(): products.reshape(group_count, block_rows * window)  66.9 us
    reduce_sum x6, other arithmetic, feat_grads(): jnp.sum(jnp.where(same_doc, source * grads.astype(jnp.float32), 0.0), axi...  44.1 us
    while x38, local copies, waits for them, and re-layouts  30.7 us
  transfers between devices with their start and end apart: 9, of which 1 were waited for; matrix products, arithmetic and copies ran while one was open for 37% of the time, Pallas kernels for 0%

commit v1 on v0

v1 whole, which is shorter than its diff:
```python
import functools

import jax
import jax.numpy as jnp
from jax import lax
from jax.experimental import pallas as pl
from jax.experimental.pallas import tpu as pltpu
from jax.sharding import PartitionSpec as P

LANES = 128
PAD = 8
STRIP = 64
CHUNKS = 2
WIDE = 512
BF = jnp.bfloat16
F32 = jnp.float32


def shift(value, axis, steps):
    count = lax.axis_size(axis)
    pairs = [(s, s + steps) for s in range(count) if 0 <= s + steps < count]
    return lax.ppermute(value, axis, pairs)


def iota(shape, dim):
    return lax.broadcasted_iota(jnp.int32, shape, dim)


def fill_dist(scal, docs, dist_ref):
    rows = dist_ref.shape[0]
    pos = iota((rows, LANES), 0)
    start = jnp.full((rows, LANES), -(2**20), jnp.int32)
    for k in range(docs):
        edge = scal[2 + k] - scal[0]
        start = jnp.where(edge <= pos, jnp.maximum(start, edge), start)
    dist_ref[...] = pos - start


def crosses(scal, docs, first, last):
    hit = False
    for k in range(docs):
        edge = scal[2 + k] - scal[0]
        hit = jnp.logical_or(hit, jnp.logical_and(edge > first, edge <= last))
    return hit


def either(cond, body):
    @pl.when(cond)
    def _():
        body(True)

    @pl.when(jnp.logical_not(cond))
    def _():
        body(False)


def featurize_kernel(
    docs, short, scal, q_ref, k_ref, v_ref, og_ref, halo_ref, taps_ref,
    query_ref, keys_ref, values_ref, mix_ref, mgr_ref, tail_ref, head_ref,
    dist, ext, mixed,
):
    rows, width = q_ref.shape
    filled = scal[1]
    edge_rows = tail_ref.shape[0]

    @pl.when(pl.program_id(0) == 0)
    def _():
        fill_dist(scal, docs, dist)

    def tile(t, carry):
        cols = pl.ds(pl.multiple_of(t * LANES, LANES), LANES)
        halo = halo_ref[:, cols].astype(F32)
        for w, ref in enumerate((q_ref, k_ref, v_ref)):
            ext[w, 0:PAD, :] = halo[w * PAD : (w + 1) * PAD]
            ext[w, PAD : PAD + rows, :] = ref[:, cols].astype(F32)
        for r0 in range(0, rows, STRIP):
            span = slice(r0, r0 + STRIP)

            def strip(masked, r0=r0, span=span):
                outs = []
                for w in range(3):
                    acc = None
                    for j in range(short):
                        source = ext[w, PAD + r0 - j : PAD + r0 - j + STRIP, :]
                        term = taps_ref[w * short + j : w * short + j + 1, cols] * source
                        if masked and j:
                            term = jnp.where(dist[span, :] >= j, term, 0.0)
                        acc = term if acc is None else acc + term
                    outs.append(acc)
                query, keys, values = outs
                query_ref[span, cols] = query.astype(BF)
                keys_ref[span, cols] = keys.astype(BF)
                values_ref[span, cols] = values.astype(BF)
                mix = (keys * values).astype(BF)
                mix_ref[span, cols] = mix
                mixed[span, :] = mix.astype(F32)
                valid = iota((STRIP, LANES), 0) + r0 < filled
                mgr = jnp.where(valid, og_ref[span, cols].astype(F32) * query, 0.0).astype(BF)
                mgr_ref[span, cols] = mgr
                if r0 < edge_rows:
                    head_ref[span, cols] = mgr

            either(crosses(scal, docs, r0 - PAD, r0 + STRIP + PAD), strip)
        tail_ref[:, cols] = mixed[pl.ds(filled - edge_rows, edge_rows), :].astype(BF)
        return carry

    lax.fori_loop(0, width // LANES, tile, 0)


def pair_mask(scal, docs, shape, p_dim, p0, s0, taps):
    p = iota(shape, p_dim) + p0
    s = iota(shape, 1 - p_dim) + s0
    lag = p - s
    keep = jnp.where(jnp.logical_and(lag >= 0, lag < taps), 1.0, 0.0)
    for k in range(docs):
        edge = scal[2 + k] - scal[0]
        keep = jnp.where(jnp.logical_and(s < edge, edge <= p), 0.0, keep)
    return keep


def mix_kernel(
    docs, short, per_group, scal, prev_ref, mix_ref, mgr_ref, next_ref, query_ref, keys_ref,
    values_ref, og_ref, q_ref, k_ref, v_ref, halo_ref, hfwd_ref, hrev_ref, skip_ref, *rest,
):
    hyena_ref, qb_ref, kb_ref, vb_ref, head_ref, tapg_ref, feat_ref = rest[-19:-12]
    dist, m_fwd, m_bwd, m_lag, ext, xs, gext, gs, lhs, yacc, bacc, facc = rest[-12:]
    rows, width = mix_ref.shape
    taps = LANES
    blocks = rows // taps
    filled = scal[1]
    groups = LANES // per_group
    square = (taps, taps)

    @pl.when(pl.program_id(0) == 0)
    def _():
        fill_dist(scal, docs, dist)
        for b in range(blocks):
            for half in range(2):
                keep = pair_mask(scal, docs, square, 0, b * taps, (b - 1 + half) * taps, taps)
                m_fwd[b, :, half * taps : (half + 1) * taps] = keep.astype(BF)
                m_lag[b, :, half * taps : (half + 1) * taps] = keep
                keep = pair_mask(scal, docs, square, 1, (b + half) * taps, b * taps, taps)
                m_bwd[b, :, half * taps : (half + 1) * taps] = keep.astype(BF)

    def tile(t, carry):
        cols = pl.ds(pl.multiple_of(t * LANES, LANES), LANES)
        halo = halo_ref[:, cols].astype(F32)
        for w, ref in enumerate((q_ref, k_ref, v_ref)):
            ext[w, 0:PAD, :] = halo[w * PAD : (w + 1) * PAD]
            ext[w, PAD : PAD + rows, :] = ref[:, cols].astype(F32)
        xs[0:taps, :] = prev_ref[:, cols]
        xs[taps : taps + rows, :] = mix_ref[:, cols]
        gext[0:rows, :] = mgr_ref[:, cols].astype(F32)
        gext[rows : rows + taps, :] = jnp.zeros(square, F32)
        gext[pl.ds(filled, taps), :] = next_ref[:, cols].astype(F32)
        gs[...] = gext[...].astype(BF)
        group_of = iota((taps, LANES), 1) // per_group

        for g in range(groups):
            row = t * groups + g
            crev = pltpu.roll(
                jnp.broadcast_to(hrev_ref[pl.ds(row, 1), :], square), 0, 1, stride=1, stride_axis=0
            ).astype(BF)
            cfwd = pltpu.roll(
                jnp.broadcast_to(hfwd_ref[pl.ds(row, 1), :], square), 0, 1, stride=1, stride_axis=0
            ).astype(BF)
            crev2 = jnp.concatenate([crev, crev], axis=1)
            cfwd2 = jnp.concatenate([cfwd, cfwd], axis=1)
            mine = group_of == g
            total = None
            for b in range(blocks):
                out = jnp.dot(
                    crev2 * m_fwd[b], xs[b * taps : (b + 2) * taps, :], preferred_element_type=F32
                )
                here = slice(b * taps, (b + 1) * taps)
                yacc[here, :] = out if g == 0 else jnp.where(mine, out, yacc[here, :])
                out = jnp.dot(
                    cfwd2 * m_bwd[b], gs[b * taps : (b + 2) * taps, :], preferred_element_type=F32
                )
                bacc[here, :] = out if g == 0 else jnp.where(mine, out, bacc[here, :])
                own = jnp.where(mine, mgr_ref[here, cols], jnp.zeros((), BF))
                prod = lax.dot_general(
                    own, xs[b * taps : (b + 2) * taps, :], (((1,), (1,)), ((), ())),
                    preferred_element_type=F32,
                )
                prod = prod * m_lag[b]
                prod = prod[:, :taps] + prod[:, taps:]
                total = prod if total is None else total + prod
            acc = total[0:8, :]
            for i in range(1, taps // 8):
                acc = acc + pltpu.roll(total[8 * i : 8 * i + 8, :], taps - 8 * i, 1)
            sub = iota((8, LANES), 0)
            for bit in (1, 2, 4):
                acc = jnp.where((sub & bit) != 0, pltpu.roll(acc, taps - bit, 1), acc)
            tapg_ref[pl.ds(row, 1), :] = jnp.sum(acc, axis=0, keepdims=True)

        facc[...] = jnp.zeros_like(facc)
        skip = skip_ref[:, cols]
        for r0 in range(0, rows, STRIP):
            span = slice(r0, r0 + STRIP)
            valid = iota((STRIP, LANES), 0) + r0 < filled
            mix = mix_ref[span, cols].astype(F32)
            mgr = mgr_ref[span, cols].astype(F32)
            gated = yacc[span, :] + skip * mix
            back = bacc[span, :] + skip * mgr
            hyena_ref[span, cols] = jnp.where(
                valid, query_ref[span, cols].astype(F32) * gated, 0.0
            ).astype(BF)
            qb = jnp.where(valid, og_ref[span, cols].astype(F32) * gated, 0.0).astype(BF)
            kb = jnp.where(valid, back * values_ref[span, cols].astype(F32), 0.0).astype(BF)
            vb = jnp.where(valid, back * keys_ref[span, cols].astype(F32), 0.0).astype(BF)
            qb_ref[span, cols] = qb
            kb_ref[span, cols] = kb
            vb_ref[span, cols] = vb
            grads = [qb.astype(F32), kb.astype(F32), vb.astype(F32)]
            if r0 == 0:
                for w in range(3):
                    head_ref[w * PAD : (w + 1) * PAD, cols] = grads[w][0:PAD].astype(BF)

            def rows_sum(value):
                return jnp.sum(value.reshape(STRIP // 8, 8, LANES), axis=0)

            last = 3 * short * 8
            facc[last : last + 8, :] += rows_sum(mix * mgr)

            def strip(masked, r0=r0, span=span, grads=grads):
                for w in range(3):
                    for j in range(short):
                        source = ext[w, PAD + r0 - j : PAD + r0 - j + STRIP, :]
                        term = source * grads[w]
                        if masked and j:
                            term = jnp.where(dist[span, :] >= j, term, 0.0)
                        at = (w * short + j) * 8
                        facc[at : at + 8, :] += rows_sum(term)

            either(crosses(scal, docs, r0 - PAD, r0 + STRIP + PAD), strip)
        slots = feat_ref.shape[0] // (width // LANES)
        summed = jnp.sum(facc[...].reshape(slots, 8, LANES), axis=1)
        feat_ref[pl.ds(pl.multiple_of(t * slots, slots), slots), :] = summed
        return carry

    lax.fori_loop(0, width // LANES, tile, 0)


def unfeaturize_kernel(docs, short, scal, qb_ref, kb_ref, vb_ref, halo_ref, taps_ref, *rest):
    outs = rest[-5:-2]
    dist, ext = rest[-2:]
    rows, width = qb_ref.shape
    filled = scal[1]

    @pl.when(pl.program_id(0) == 0)
    def _():
        fill_dist(scal, docs, dist)

    def tile(t, carry):
        cols = pl.ds(pl.multiple_of(t * LANES, LANES), LANES)
        halo = halo_ref[:, cols].astype(F32)
        for w, ref in enumerate((qb_ref, kb_ref, vb_ref)):
            ext[w, 0:rows, :] = ref[:, cols].astype(F32)
            ext[w, pl.ds(filled, PAD), :] = halo[w * PAD : (w + 1) * PAD]
        for r0 in range(0, rows, STRIP):
            span = slice(r0, r0 + STRIP)

            def strip(masked, r0=r0, span=span):
                valid = iota((STRIP, LANES), 0) + r0 < filled
                for w in range(3):
                    acc = None
                    for j in range(short):
                        source = ext[w, r0 + j : r0 + j + STRIP, :]
                        term = taps_ref[w * short + j : w * short + j + 1, cols] * source
                        if masked and j:
                            term = jnp.where(dist[r0 + j : r0 + j + STRIP, :] >= j, term, 0.0)
                        acc = term if acc is None else acc + term
                    outs[w][span, cols] = jnp.where(valid, acc, 0.0).astype(BF)

            either(crosses(scal, docs, r0 - PAD, r0 + STRIP + PAD), strip)
        return carry

    lax.fori_loop(0, width // LANES, tile, 0)


def call(kernel, grid, ins, outs, scratch, args, scal, aliases=None, cost=None):
    specs = pltpu.PrefetchScalarGridSpec(
        num_scalar_prefetch=1, grid=grid, in_specs=[s for s in ins],
        out_specs=[s for s, _ in outs], scratch_shapes=scratch,
    )
    return pl.pallas_call(
        kernel, grid_spec=specs, out_shape=[o for _, o in outs],
        input_output_aliases=aliases or {},
        compiler_params=pltpu.CompilerParams(
            dimension_semantics=("arbitrary",), vmem_limit_bytes=56 * 1024 * 1024
        ),
        cost_estimate=cost,
    )(scal, *args)


def shards(
    query_in, key_in, value_in, out_grad, fill_counts, doc_starts, feat_taps, mix_taps, skip_gain
):
    rows, channels = query_in.shape
    short = feat_taps.shape[1]
    groups, taps = mix_taps.shape
    docs = doc_starts.shape[0]
    per_group = channels // groups
    shard_count, mine = lax.axis_size("ctx"), lax.axis_index("ctx")
    filled = fill_counts[0]

    def tail_rows(source):
        return lax.dynamic_slice_in_dim(source, filled - PAD, PAD, 0)

    tails = jnp.concatenate([tail_rows(s) for s in (query_in, key_in, value_in)], axis=0)
    halo = shift(tails, "ctx", 1)
    counts = lax.all_gather(fill_counts, "ctx", tiled=True)
    first = jnp.sum(jnp.where(jnp.arange(shard_count) < mine, counts, 0))
    scal = jnp.concatenate([first[None], fill_counts, doc_starts]).astype(jnp.int32)

    slots = 3 * short + 1
    slots = slots + (-slots) % 8
    taps_all = jnp.pad(feat_taps.reshape(3 * short, channels).astype(F32), ((0, slots - 3 * short), (0, 0)))
    hfwd = mix_taps.astype(F32)
    hrev = jnp.concatenate([hfwd[:, :1], hfwd[:, :0:-1]], axis=1)
    skip = skip_gain[None, :]

    chunks = CHUNKS
    per_chunk = channels // chunks
    wide = min(WIDE, per_chunk)
    steps = per_chunk // wide
    tiles = wide // LANES
    bf = lambda *shape: jax.ShapeDtypeStruct(shape, BF)
    f32 = lambda *shape: jax.ShapeDtypeStruct(shape, F32)

    def cols(height, offset=0):
        return pl.BlockSpec((height, wide), lambda i, s: (0, i + offset))

    featured, sent_mix, sent_grad = [], [], []
    for c in range(chunks):
        off = c * steps
        full = cols(rows, off)
        outs = call(
            functools.partial(featurize_kernel, docs, short), (steps,),
            [full] * 4 + [cols(3 * PAD, off), cols(slots, off)],
            [(cols(rows), bf(rows, per_chunk))] * 5 + [(cols(taps), bf(taps, per_chunk))] * 2,
            [
                pltpu.VMEM((rows, LANES), jnp.int32),
                pltpu.VMEM((3, PAD + rows, LANES), F32),
                pltpu.VMEM((rows, LANES), F32),
            ],
            (query_in, key_in, value_in, out_grad, halo, taps_all), scal,
            cost=pl.CostEstimate(flops=50 * rows * per_chunk, bytes_accessed=20 * rows * per_chunk, transcendentals=0),
        )
        featured.append(outs)
        sent_mix.append(shift(outs[5], "ctx", 1))
        sent_grad.append(shift(outs[6], "ctx", -1))

    hyena = None
    backs, sent_back, tap_grads, feat_grads = [], [], [], []
    blocks = rows // taps
    for c in range(chunks):
        off = c * steps
        query, keys, values, mix, mgr = featured[c][:5]
        full = cols(rows, off)
        ins = [cols(taps), cols(rows), cols(rows), cols(taps)] + [cols(rows)] * 3 + [full] * 4
        ins += [cols(3 * PAD, off)]
        gspec = pl.BlockSpec((wide // per_group, taps), lambda i, s, off=off: (i + off, 0))
        ins += [gspec, gspec, cols(1, off)]
        args = [sent_mix[c], mix, mgr, sent_grad[c], query, keys, values, out_grad]
        args += [query_in, key_in, value_in, halo, hfwd, hrev, skip]
        aliases = None
        if hyena is not None:
            ins.append(pl.BlockSpec(memory_space=pl.ANY))
            args.append(hyena)
            aliases = {len(args): 0}
        outs = call(
            functools.partial(mix_kernel, docs, short, per_group), (steps,), ins,
            [(full, bf(rows, channels))]
            + [(cols(rows), bf(rows, per_chunk))] * 3
            + [(cols(3 * PAD), bf(3 * PAD, per_chunk))]
            + [
                (pl.BlockSpec((wide // per_group, taps), lambda i, s: (i, 0)), f32(per_chunk // per_group, taps)),
                (pl.BlockSpec((tiles * slots, LANES), lambda i, s: (i, 0)), f32(per_chunk // LANES * slots, LANES)),
            ],
            [
                pltpu.VMEM((rows, LANES), jnp.int32),
                pltpu.VMEM((blocks, taps, 2 * taps), BF),
                pltpu.VMEM((blocks, taps, 2 * taps), BF),
                pltpu.VMEM((blocks, taps, 2 * taps), F32),
                pltpu.VMEM((3, PAD + rows, LANES), F32),
                pltpu.VMEM((rows + taps, LANES), BF),
                pltpu.VMEM((rows + taps, LANES), F32),
                pltpu.VMEM((rows + taps, LANES), BF),
                pltpu.VMEM((8, LANES), BF),
                pltpu.VMEM((rows, LANES), F32),
                pltpu.VMEM((rows, LANES), F32),
                pltpu.VMEM((8 * slots, LANES), F32),
            ],
            args, scal, aliases,
            cost=pl.CostEstimate(flops=2000 * rows * per_chunk, bytes_accessed=40 * rows * per_chunk, transcendentals=0),
        )
        hyena = outs[0]
        backs.append(outs[1:4])
        sent_back.append(shift(outs[4], "ctx", -1))
        tap_grads.append(outs[5])
        feat_grads.append(outs[6])

    grads = None
    for c in range(chunks):
        off = c * steps
        ins = [cols(rows)] * 3 + [cols(3 * PAD), cols(slots, off)]
        args = list(backs[c]) + [sent_back[c], taps_all]
        aliases = None
        if grads is not None:
            for w in range(3):
                ins.append(pl.BlockSpec(memory_space=pl.ANY))
                args.append(grads[w])
            aliases = {len(args) - 2 + w: w for w in range(3)}
        grads = call(
            functools.partial(unfeaturize_kernel, docs, short), (steps,), ins,
            [(cols(rows, off), bf(rows, channels))] * 3,
            [
                pltpu.VMEM((rows + 2 * PAD, LANES), jnp.int32),
                pltpu.VMEM((3, rows + 2 * PAD, LANES), F32),
            ],
            args, scal, aliases,
            cost=pl.CostEstimate(flops=50 * rows * per_chunk, bytes_accessed=12 * rows * per_chunk, transcendentals=0),
        )

    payload = jnp.concatenate(feat_grads + tap_grads, axis=0)
    lines = payload.shape[0]
    extra = (-lines) % shard_count
    payload = jnp.pad(payload, ((0, extra), (0, 0))).astype(BF)
    share = payload.shape[0] // shard_count
    pieces = lax.all_to_all(payload, "ctx", 0, 0, tiled=True)
    summed = jnp.sum(pieces.reshape(shard_count, share, LANES).astype(F32), axis=0).astype(BF)
    spread = jnp.broadcast_to(summed[None], (shard_count, share, LANES)).reshape(-1, LANES)
    whole = lax.all_to_all(spread, "ctx", 0, 0, tiled=True)[:lines].astype(F32)
    total_params = (groups * taps + channels * (1 + 3 * short)) * lax.axis_size("tp")
    whole_sq = lax.psum(jnp.sum(whole * whole), "tp")
    factor = lax.rsqrt(whole_sq / total_params + 1e-06)
    scaled = whole * factor
    split = channels // LANES * slots
    mix_part = scaled[split:]
    mix_out = jnp.concatenate([mix_part[:, :1], mix_part[:, :0:-1]], axis=1)
    feat = scaled[:split].reshape(channels // LANES, slots, LANES).transpose(1, 0, 2).reshape(slots, channels)
    feat_out = feat[: 3 * short].reshape(3, short, channels)
    skip_out = feat[3 * short]
    return (hyena, grads[0], grads[1], grads[2], mix_out, skip_out, feat_out)


def solution(mesh):
    stream = P("ctx", "tp")
    in_specs = (
        stream, stream, stream, stream, P("ctx"), P(), P(None, None, "tp"), P("tp", None), P("tp"),
    )
    out_specs = (stream, stream, stream, stream, P("tp", None), P("tp"), P(None, None, "tp"))
    return jax.shard_map(shards, mesh=mesh, in_specs=in_specs, out_specs=out_specs, check_vma=False)
```

time: 879 us -> 196 us (0.22)
  local copies, waits for them, and re-layouts: 418 us -> 11.8 us
  other arithmetic: 137 us -> 8.27 us
  Pallas kernels: 0 us -> 108 us
  matrix products: 73.7 us -> 0 us
  blocking collectives: 102 us -> 28.9 us
  waiting for transfers between devices: 87.1 us -> 20.8 us
  between operations: 19.3 us -> 2.26 us
  loops' own time: 13.8 us -> 0 us
    reshape x4 -> x1, local copies, waits for them, and re-layouts: 180 us -> 0.8 us  [shards(): feat_out = feat[:3 * short].reshape(3, short, channels)]
    pallas_call x0 -> x6, Pallas kernels: none -> 108 us  [call(): pl.pallas_call(kernel, grid_spec=specs, out_shape=[o for _, o in outs], i...]
    reduce_sum x15 -> x3, other arithmetic: 96.2 us -> 1.41 us  [the longest x1 0.73 us: shards(): whole_sq = lax.psum(jnp.sum(whole * whole), 'tp')]
    psum x2 -> x1, blocking collectives: 90.4 us -> 3.08 us  [shards(): whole_sq = lax.psum(jnp.sum(whole * whole), 'tp')]
    psum x1 -> x0, waiting for transfers between devices: 87.1 us -> none  [shards(): taps_sum, skip_sum, feat_sum = lax.psum((taps_grad, skip_part, feat), 'ctx')]
    unnamed x223 -> x27, local copies, waits for them, and re-layouts: 89.1 us -> 6.02 us
    dot_general x6 -> x0, matrix products: 73.7 us -> none  [contract(): return jnp.einsum(form, left, right, preferred_element_type=jnp.float32)]
    dynamic_slice x41 -> x2, local copies, waits for them, and re-layouts: 36.3 us -> 1.96 us  [tail_rows(): return lax.dynamic_slice_in_dim(source, filled - PAD, PAD, 0)]
  transfers between devices with their start and end apart: 9 -> 8, of which waited for: 1 -> 2; matrix products, arithmetic and copies ran while one was open for 37% -> 4% of each run, Pallas kernels for 0% -> 27%
where the time goes in v1:
time: 196 us; the launch traced here: 198 us
  Pallas kernels  108 us (55%)
  blocking collectives  28.9 us (15%)
  waiting for transfers between devices  20.8 us (11%)
  starting transfers between devices  18.4 us (9%)
  local copies, waits for them, and re-layouts  11.8 us (6%)
  other arithmetic  8.27 us (4%)
  between operations  2.26 us (1%)
    pallas_call x6, Pallas kernels, call(): pl.pallas_call(kernel, grid_spec=specs, out_shape=[o for _, o in outs], i...  108 us
    ppermute x7, waiting for transfers between devices, shift(): return lax.ppermute(value, axis, pairs)  20.8 us
    ppermute x7, starting transfers between devices, shift(): return lax.ppermute(value, axis, pairs)  14.9 us
    unnamed x1, blocking collectives  14.7 us
    all_to_all x1, blocking collectives, shards(): pieces = lax.all_to_all(payload, 'ctx', 0, 0, tiled=True)  11.1 us
    unnamed x27, local copies, waits for them, and re-layouts  6.02 us
  transfers between devices with their start and end apart: 8, of which 2 were waited for; matrix products, arithmetic and copies ran while one was open for 4% of the time, Pallas kernels for 27%

profile of v1, /device:TPU:0, one launch (start us, length us, event | category | flops | bytes accessed | tf_op | source)
XLA Modules:
  0.0 198.1 jit_solution(6633626661335599593)
XLA Ops:
  1.3 0.9 constant_dynamic-slice_fusion.2
  2.2 1.0 constant_dynamic-slice_fusion
  3.3 4.9 %collective-permute-start = (bf16[24,4096]{1,0:T(8,128)(2,1)S(1)}, bf16[24,4096]{1,0:T(8,128)(2,1)S(1)}, u32[]{:S(2)}, u32[]{:S(2)}) collective-permute-start(bf16[24,4096]{1,0:T(8,128)(2,1)S(1)} %pad_maximum_fusion.1), channel_id=1, source_target_pairs={{0,2},{2,4},{4,6},{6,8},{8,10},{10,12},{12,14},{14,16},{16,18},{18... | collective-permute-start | bytes 589832 | tf_op jit(solution)/shard_map/ppermute | solution.py:22
  8.2 1.2 dynamic-slice
  10.2 14.7 %all-reduce.1 = s32[16]{0:T(128)S(1)} all-reduce(s32[16]{0:T(128)S(1)} %dynamic-update-slice), channel_id=1, replica_groups=mesh['ctx'=16,'tp'=2] {'ctx'}, use_global_device_ids=true, to_apply=%add.1 | all-reduce | flops 16 | bytes 128
  24.9 1.0 convert_element_type.21
  25.9 0.8 pad_convert_fusion.taps_ref
  27.3 2.0 pad_add_fusion.scal
  29.9 10.6 %shard_map.145 = (bf16[256,2048]{1,0:T(8,128)(2,1)}, bf16[256,2048]{1,0:T(8,128)(2,1)}, bf16[256,2048]{1,0:T(8,128)(2,1)}, bf16[256,2048]{1,0:T(8,128)(2,1)}, bf...) custom-call(s32[6]{0:T(128)} %pad_add_fusion.scal, bf16[256,4096]{1,0:T(8,128)(2,1)} %q_ref.7, ...), custom_call_target="tpu_custom_call" | custom-call | flops 26214400 | bytes 10485760 | tf_op jit(solution)/shard_map/pallas_call | solution.py:287
  40.5 1.3 collective-permute-start.3
  41.8 1.4 collective-permute-start.4
  43.3 10.6 %shard_map.144 = (bf16[256,2048]{1,0:T(8,128)(2,1)}, bf16[256,2048]{1,0:T(8,128)(2,1)}, bf16[256,2048]{1,0:T(8,128)(2,1)}, bf16[256,2048]{1,0:T(8,128)(2,1)}, bf...) custom-call(s32[6]{0:T(128)} %pad_add_fusion.scal, bf16[256,4096]{1,0:T(8,128)(2,1)} %q_ref.7, ...), custom_call_target="tpu_custom_call" | custom-call | flops 26214400 | bytes 10485760 | tf_op jit(solution)/shard_map/pallas_call | solution.py:287
  53.9 3.4 %collective-permute-start.1 = (bf16[128,2048]{1,0:T(8,128)(2,1)}, bf16[128,2048]{1,0:T(8,128)(2,1)S(1)}, u32[]{:S(2)}, u32[]{:S(2)}) collective-permute-start(bf16[128,2048]{1,0:T(8,128)(2,1)} %get-tuple-element.41), channel_id=1, source_target_pairs={{0,2},{2,4},{4,6},{6,8},{8,10},{10,12},{12,14},{14,16},{16,18},{18... | collective-permute-start | bytes 1572872 | tf_op jit(solution)/shard_map/ppermute | solution.py:22
  57.3 1.3 collective-permute-start.2
  59.5 0.8 pad_maximum_fusion.2.hrev_ref
  60.3 16.6 %collective-permute-done.3.prev_ref = bf16[128,2048]{1,0:T(8,128)(2,1)S(1)} collective-permute-done((bf16[128,2048]{1,0:T(8,128)(2,1)}, bf16[128,2048]{1,0:T(8,128)(2,1)S(1)}, u32[]{:S(2)}, u32[]{:S(2)}) %collective-permute-start.3) | collective-permute-done | bytes 524320 | tf_op jit(solution)/shard_map/ppermute | solution.py:22
  76.9 0.8 copy-done.4
  77.9 33.0 %shard_map.146 = (bf16[256,4096]{1,0:T(8,128)(2,1)}, bf16[256,2048]{1,0:T(8,128)(2,1)}, bf16[256,2048]{1,0:T(8,128)(2,1)}, bf16[256,2048]{1,0:T(8,128)(2,1)}, bf...) custom-call(s32[6]{0:T(128)} %pad_add_fusion.scal, bf16[128,2048]{1,0:T(8,128)(2,1)} %copy-done.4, ...), custom_call_target="tpu_custom_call" | custom-call | flops 1048576000 | bytes 20971520 | tf_op jit(solution)/shard_map/pallas_call | solution.py:287
  110.9 0.8 copy-done.2
  112.0 33.2 %shard_map.147 = (bf16[256,4096]{1,0:T(8,128)(2,1)}, bf16[256,2048]{1,0:T(8,128)(2,1)}, bf16[256,2048]{1,0:T(8,128)(2,1)}, bf16[256,2048]{1,0:T(8,128)(2,1)}, bf...) custom-call(s32[6]{0:T(128)} %pad_add_fusion.scal, ...), custom_call_target="tpu_custom_call", output_to_operand_aliasing={{0}: (16, {})} | custom-call | flops 1048576000 | bytes 20971520 | tf_op jit(solution)/shard_map/pallas_call | solution.py:287
  145.2 1.0 convert.17
  146.2 0.8 convert.19
  147.1 11.1 %all_to_all.12 = bf16[16,64,128]{2,1,0:T(8,128)(2,1)S(1)} all-to-all(bf16[16,64,128]{2,1,0:T(8,128)(2,1)S(1)} %bitcast.16), channel_id=1, replica_groups=mesh['ctx'=16,'tp'=2] {'ctx'}, dimensions={0} | all-to-all | bytes 524288 | tf_op jit(solution)/shard_map/all_to_all | solution.py:432
  159.0 3.5 %all-to-all-start.1 = ((bf16[16,64,128]{2,1,0:T(8,128)(2,1)}), bf16[16,64,128]{2,1,0:T(8,128)(2,1)S(1)}, u32[]{:S(2)}, u32[]{:S(2)}) async-start(bf16[16,64,128]{2,1,0:T(8,128)(2,1)} %broadcast_in_dim.19), calls=%async_computation.1 | async-start | bytes 524288 | tf_op jit(solution)/shard_map/all_to_all | solution.py:435
  162.5 1.3 collective-permute-start.6
  163.8 1.3 collective-permute-start.5
  165.1 4.2 %collective-permute-done.6.halo_ref = bf16[24,2048]{1,0:T(8,128)(2,1)S(1)} collective-permute-done((bf16[24,2048]{1,0:T(8,128)(2,1)S(1)}, bf16[24,2048]{1,0:T(8,128)(2,1)S(1)}, u32[]{:S(2)}, u32[]{:S(2)}) %collective-permute-start.6) | collective-permute-done | bytes 98336 | tf_op jit(solution)/shard_map/ppermute | solution.py:22
  170.0 10.1 %shard_map.148 = (bf16[256,4096]{1,0:T(8,128)(2,1)}, bf16[256,4096]{1,0:T(8,128)(2,1)}, bf16[256,4096]{1,0:T(8,128)(2,1)}) custom-call(s32[6]{0:T(128)} %pad_add_fusion.scal, bf16[256,2048]{1,0:T(8,128)(2,1)} %get-tuple-element.61.qb_ref, bf16[256,2048]{1,0:T(8,128)(2,1)} %get-tuple-element.62.kb_ref, bf16[256,2048]{1,0:T(8,128)(2,1)} %get-tuple-element.63.vb_ref, ...), custom_call_target="tpu_custom_call" | custom-call | flops 26214400 | bytes 6291456 | tf_op jit(solution)/shard_map/pallas_call | solution.py:287
  181.5 10.2 %shard_map.149 = (bf16[256,4096]{1,0:T(8,128)(2,1)}, bf16[256,4096]{1,0:T(8,128)(2,1)}, bf16[256,4096]{1,0:T(8,128)(2,1)}) custom-call(s32[6]{0:T(128)} %pad_add_fusion.scal, bf16[256,2048]{1,0:T(8,128)(2,1)} %get-tuple-element.57.qb_ref, bf16[256,2048]{1,0:T(8,128)(2,1)} %get-tuple-element.58.kb_ref, ...), custom_call_target="tpu_custom_call", output_to_operand_aliasing={{0}: (6, {}), {1}: (7, {}), {2}: (8, {})} | custom-call | flops 26214400 | bytes 6291456 | tf_op jit(solution)/shard_map/pallas_call | solution.py:287
  191.7 3.1 %psum.7 = f32[]{:T(128)} all-reduce(f32[]{:T(128)} %fusion), channel_id=1, replica_groups=mesh['ctx'=16,'tp'=2] {'tp'}, use_global_device_ids=true, to_apply=%region_3.4 | all-reduce | flops 1 | bytes 8 | tf_op jit(solution)/shard_map/psum | solution.py:437
  196.4 0.8 reshape.49
  197.3 0.8 pad_maximum_fusion.3
  (49 shorter events, 7.4 us)
Async XLA Ops:
  3.3 26.0 %collective-permute-start = (bf16[24,4096]{1,0:T(8,128)(2,1)S(1)}, bf16[24,4096]{1,0:T(8,128)(2,1)S(1)}, u32[]{:S(2)}, u32[]{:S(2)}) collective-permute-start(bf16[24,4096]{1,0:T(8,128)(2,1)S(1)} %pad_maximum_fusion.1), channel_id=1, source_target_pairs={{0,2},{2,4},{4,6},{6,8},{8,10},{10,12},{12,14},{14,16},{16,18},{18... | collective-permute-start | bytes 589832 | tf_op jit(solution)/shard_map/ppermute | solution.py:22
  29.2 0.7 copy-start
  40.5 36.4 %collective-permute-start.3 = (bf16[128,2048]{1,0:T(8,128)(2,1)}, bf16[128,2048]{1,0:T(8,128)(2,1)S(1)}, u32[]{:S(2)}, u32[]{:S(2)}) collective-permute-start(bf16[128,2048]{1,0:T(8,128)(2,1)} %get-tuple-element.48), channel_id=1, source_target_pairs={{0,2},{2,4},{4,6},{6,8},{8,10},{10,12},{12,14},{14,16},{16,18},{18... | collective-permute-start | bytes 1572872 | tf_op jit(solution)/shard_map/ppermute | solution.py:22
  41.8 16.7 %copy-start.1 = (bf16[256,128]{1,0:T(8,128)(2,1)S(1)}, bf16[256,128]{1,0:T(8,128)(2,1)}, u32[]{:S(2)}) copy-start(bf16[256,128]{1,0:T(8,128)(2,1)} %param.16) | copy-start | bytes 196612
  41.8 35.0 %collective-permute-start.4 = (bf16[128,2048]{1,0:T(8,128)(2,1)}, bf16[128,2048]{1,0:T(8,128)(2,1)S(1)}, u32[]{:S(2)}, u32[]{:S(2)}) collective-permute-start(bf16[128,2048]{1,0:T(8,128)(2,1)} %get-tuple-element.51), channel_id=1, source_target_pairs={{2,0},{4,2},{6,4},{8,6},{10,8},{12,10},{14,12},{16,14},{18,16},{20... | collective-permute-start | bytes 1572872 | tf_op jit(solution)/shard_map/ppermute | solution.py:22
  53.9 57.0 %collective-permute-start.1 = (bf16[128,2048]{1,0:T(8,128)(2,1)}, bf16[128,2048]{1,0:T(8,128)(2,1)S(1)}, u32[]{:S(2)}, u32[]{:S(2)}) collective-permute-start(bf16[128,2048]{1,0:T(8,128)(2,1)} %get-tuple-element.41), channel_id=1, source_target_pairs={{0,2},{2,4},{4,6},{6,8},{8,10},{10,12},{12,14},{14,16},{16,18},{18... | collective-permute-start | bytes 1572872 | tf_op jit(solution)/shard_map/ppermute | solution.py:22
  57.3 53.7 %collective-permute-start.2 = (bf16[128,2048]{1,0:T(8,128)(2,1)}, bf16[128,2048]{1,0:T(8,128)(2,1)S(1)}, u32[]{:S(2)}, u32[]{:S(2)}) collective-permute-start(bf16[128,2048]{1,0:T(8,128)(2,1)} %get-tuple-element.44), channel_id=1, source_target_pairs={{2,0},{4,2},{6,4},{8,6},{10,8},{12,10},{14,12},{16,14},{18,16},{20... | collective-permute-start | bytes 1572872 | tf_op jit(solution)/shard_map/ppermute | solution.py:22
  76.9 0.8 copy-start.4
  76.9 1.0 copy-start.5
  110.9 0.8 copy-start.2
  110.9 1.1 copy-start.3
  112.0 35.0 %copy-start.6 = (f32[384,128]{1,0:T(8,128)S(1)}, f32[384,128]{1,0:T(8,128)}, u32[]{:S(2)}) copy-start(f32[384,128]{1,0:T(8,128)} %get-tuple-element.71) | copy-start | bytes 589828
  112.0 35.0 %copy-start.9 = (f32[128,128]{1,0:T(8,128)S(1)}, f32[128,128]{1,0:T(8,128)}, u32[]{:S(2)}) copy-start(f32[128,128]{1,0:T(8,128)} %get-tuple-element.73) | copy-start | bytes 196612
  145.2 17.4 %copy-start.10 = (bf16[24,2048]{1,0:T(8,128)(2,1)S(1)}, bf16[24,2048]{1,0:T(8,128)(2,1)}, u32[]{:S(2)}) copy-start(bf16[24,2048]{1,0:T(8,128)(2,1)} %get-tuple-element.64) | copy-start | bytes 294916
  145.2 18.7 %copy-start.11 = (bf16[24,2048]{1,0:T(8,128)(2,1)S(1)}, bf16[24,2048]{1,0:T(8,128)(2,1)}, u32[]{:S(2)}) copy-start(bf16[24,2048]{1,0:T(8,128)(2,1)} %get-tuple-element.60) | copy-start | bytes 294916
  159.0 21.2 %all-to-all-start.1 = ((bf16[16,64,128]{2,1,0:T(8,128)(2,1)}), bf16[16,64,128]{2,1,0:T(8,128)(2,1)S(1)}, u32[]{:S(2)}, u32[]{:S(2)}) async-start(bf16[16,64,128]{2,1,0:T(8,128)(2,1)} %broadcast_in_dim.19), calls=%async_computation.1 | async-start | bytes 524288 | tf_op jit(solution)/shard_map/all_to_all | solution.py:435
  162.5 6.8 %collective-permute-start.6 = (bf16[24,2048]{1,0:T(8,128)(2,1)S(1)}, bf16[24,2048]{1,0:T(8,128)(2,1)S(1)}, u32[]{:S(2)}, u32[]{:S(2)}) collective-permute-start(bf16[24,2048]{1,0:T(8,128)(2,1)S(1)} %copy-done.10), channel_id=1, source_target_pairs={{2,0},{4,2},{6,4},{8,6},{10,8},{12,10},{14,12},{16,14},{18,16},{20... | collective-permute-start | bytes 294920 | tf_op jit(solution)/shard_map/ppermute | solution.py:22
  163.8 17.0 %collective-permute-start.5 = (bf16[24,2048]{1,0:T(8,128)(2,1)S(1)}, bf16[24,2048]{1,0:T(8,128)(2,1)S(1)}, u32[]{:S(2)}, u32[]{:S(2)}) collective-permute-start(bf16[24,2048]{1,0:T(8,128)(2,1)S(1)} %copy-done.11), channel_id=1, source_target_pairs={{2,0},{4,2},{6,4},{8,6},{10,8},{12,10},{14,12},{16,14},{18,16},{20... | collective-permute-start | bytes 294920 | tf_op jit(solution)/shard_map/ppermute | solution.py:22
  169.4 0.6 copy-start.8
  180.9 0.6 copy-start.7

commit v2 on v1

v2 whole, which is shorter than its diff:
```python
import functools
import math

import jax
import jax.numpy as jnp
from jax import lax
from jax.experimental import pallas as pl
from jax.experimental.pallas import tpu as pltpu
from jax.sharding import PartitionSpec as P


LANES = 128
PAD = 8
STRIP = 64
EARLY = 3
WIDE = 512
BF = jnp.bfloat16
F32 = jnp.float32


def shift(value, axis, steps):
    count = lax.axis_size(axis)
    pairs = [(s, s + steps) for s in range(count) if 0 <= s + steps < count]
    return lax.ppermute(value, axis, pairs)


def iota(shape, dim):
    return lax.broadcasted_iota(jnp.int32, shape, dim)


class Layout:
    def __init__(self, firsts, facts):
        self.firsts, self.facts = firsts, facts

    def __getitem__(self, at):
        return self.facts[at] if at else self.firsts[self.facts[0]]


def fill_dist(scal, docs, dist_ref):
    rows = dist_ref.shape[0]
    pos = iota((rows, LANES), 0)
    start = jnp.full((rows, LANES), -(2**20), jnp.int32)
    for k in range(docs):
        edge = scal[2 + k] - scal[0]
        start = jnp.where(edge <= pos, jnp.maximum(start, edge), start)
    dist_ref[...] = pos - start


def crosses(scal, docs, first, last):
    hit = False
    for k in range(docs):
        edge = scal[2 + k] - scal[0]
        hit = jnp.logical_or(hit, jnp.logical_and(edge > first, edge <= last))
    return hit


def either(cond, body):
    @pl.when(cond)
    def _():
        body(True)

    @pl.when(jnp.logical_not(cond))
    def _():
        body(False)


def featurize_kernel(
    docs, short, firsts, facts, q_ref, k_ref, v_ref, og_ref, halo_ref, taps_ref,
    query_ref, keys_ref, values_ref, mix_ref, mgr_ref, tail_ref, head_ref,
    dist, ext, mixed,
):
    scal = Layout(firsts, facts)
    rows, width = q_ref.shape
    filled = scal[1]
    edge_rows = tail_ref.shape[0]

    @pl.when(pl.program_id(0) == 0)
    def _():
        fill_dist(scal, docs, dist)

    def tile(t, carry):
        cols = pl.ds(pl.multiple_of(t * LANES, LANES), LANES)
        taps_of = [taps_ref[w, :, cols].astype(F32) for w in range(3)]
        halo = halo_ref[:, cols].astype(F32)
        for w, ref in enumerate((q_ref, k_ref, v_ref)):
            ext[w, 0:PAD, :] = halo[w * PAD : (w + 1) * PAD]
            ext[w, PAD : PAD + rows, :] = ref[:, cols].astype(F32)
        for r0 in range(0, rows, STRIP):
            span = slice(r0, r0 + STRIP)

            def strip(masked, r0=r0, span=span):
                outs = []
                for w in range(3):
                    acc = None
                    for j in range(short):
                        source = ext[w, PAD + r0 - j : PAD + r0 - j + STRIP, :]
                        term = taps_of[w][j : j + 1, :] * source
                        if masked and j:
                            term = jnp.where(dist[span, :] >= j, term, 0.0)
                        acc = term if acc is None else acc + term
                    outs.append(acc)
                query, keys, values = outs
                query_ref[span, cols] = query.astype(BF)
                keys_ref[span, cols] = keys.astype(BF)
                values_ref[span, cols] = values.astype(BF)
                mix = (keys * values).astype(BF)
                mix_ref[span, cols] = mix
                mixed[span, :] = mix.astype(F32)
                valid = iota((STRIP, LANES), 0) + r0 < filled
                mgr = jnp.where(valid, og_ref[span, cols].astype(F32) * query, 0.0).astype(BF)
                mgr_ref[span, cols] = mgr
                if r0 < edge_rows:
                    head_ref[span, cols] = mgr

            either(crosses(scal, docs, r0 - PAD, r0 + STRIP + PAD), strip)
        tail_ref[:, cols] = mixed[pl.ds(filled - edge_rows, edge_rows), :].astype(BF)
        return carry

    lax.fori_loop(0, width // LANES, tile, 0)


def pair_mask(scal, docs, shape, p_dim, p0, s0, taps):
    p = iota(shape, p_dim) + p0
    s = iota(shape, 1 - p_dim) + s0
    lag = p - s
    keep = jnp.where(jnp.logical_and(lag >= 0, lag < taps), 1.0, 0.0)
    for k in range(docs):
        edge = scal[2 + k] - scal[0]
        keep = jnp.where(jnp.logical_and(s < edge, edge <= p), 0.0, keep)
    return keep


def mix_kernel(
    docs, short, per_group, firsts, facts, prev_ref, mix_ref, mgr_ref, next_ref, query_ref, keys_ref,
    values_ref, og_ref, q_ref, k_ref, v_ref, halo_ref, hfwd_ref, hrev_ref, skip_ref, *rest,
):
    hyena_ref, sums_ref, head_ref, qb_ref, kb_ref, vb_ref = rest[-18:-12]
    m_fwd, m_bwd, m_lag, ext, xs, gext, gs, yacc, bacc, facc, back_rows, tacc = rest[-12:]
    scal = Layout(firsts, facts)
    rows, width = mix_ref.shape
    taps = LANES
    blocks = rows // taps
    filled = scal[1]
    groups = LANES // per_group
    square = (taps, taps)

    @pl.when(pl.program_id(0) == 0)
    def _():
        facc[...] = jnp.zeros_like(facc)
        for end in (0, PAD + rows):
            back_rows[:, end : end + PAD, :] = jnp.zeros((3, PAD, LANES), F32)
        for end in (0, 2 * PAD + rows):
            ext[:, :, end : end + PAD, :] = jnp.zeros((2, 3, PAD, LANES), F32)
        for b in range(blocks):
            for half in range(2):
                keep = pair_mask(scal, docs, square, 0, b * taps, (b - 1 + half) * taps, taps)
                m_fwd[b, :, half * taps : (half + 1) * taps] = keep.astype(BF)
                m_lag[b] = keep if half == 0 else m_lag[b] + keep
                keep = pair_mask(scal, docs, square, 1, (b + half) * taps, b * taps, taps)
                m_bwd[b, :, half * taps : (half + 1) * taps] = keep.astype(BF)

    piece = rows // groups
    count = width // LANES
    skips = 3 * short * 8

    def columns(t):
        return pl.ds(pl.multiple_of(t * LANES, LANES), LANES)

    def setup(t, slot):
        cols = columns(t)
        halo = halo_ref[:, cols].astype(F32)
        for w, ref in enumerate((q_ref, k_ref, v_ref)):
            ext[slot, w, PAD : 2 * PAD, :] = halo[w * PAD : (w + 1) * PAD]
            ext[slot, w, 2 * PAD : 2 * PAD + rows, :] = ref[:, cols].astype(F32)
        xs[0:taps, :] = prev_ref[:, cols]
        xs[taps : taps + rows, :] = mix_ref[:, cols]
        gext[0:rows, :] = mgr_ref[:, cols].astype(F32)
        gext[rows : rows + taps, :] = jnp.zeros(square, F32)
        gext[pl.ds(filled, taps), :] = next_ref[:, cols].astype(F32)
        gs[...] = gext[...].astype(BF)

    def circulant(ref, row):
        line = jnp.broadcast_to(ref[pl.ds(row, 1), :], square)
        return pltpu.roll(line, 0, 1, stride=1, stride_axis=0).astype(BF)

    def group(t, slot, g):
        lane_group = iota((taps, LANES), 1) // per_group
        tri = iota(square, 0) >= iota(square, 1)
        sub = iota((8, LANES), 0)
        row = t * groups + g
        mine = lane_group == g
        crev, cfwd = circulant(hrev_ref, row), circulant(hfwd_ref, row)
        crev2 = jnp.concatenate([crev, crev], axis=1)
        cfwd2 = jnp.concatenate([cfwd, cfwd], axis=1)
        total = None
        for b in range(blocks):
            here = slice(b * taps, (b + 1) * taps)
            window = slice(b * taps, (b + 2) * taps)
            out = jnp.dot(crev2 * m_fwd[b], xs[window, :], preferred_element_type=F32)
            pltpu.store(yacc.at[slot, here, :], out, mask=mine)
            out = jnp.dot(cfwd2 * m_bwd[b], gs[window, :], preferred_element_type=F32)
            pltpu.store(bacc.at[slot, here, :], out, mask=mine)
            own = jnp.where(mine, mgr_ref[here, columns(t)], jnp.zeros((), BF))
            prod = lax.dot_general(
                own, xs[window, :], (((1,), (1,)), ((), ())), preferred_element_type=F32
            )
            prod = jnp.where(tri, prod[:, taps:], prod[:, :taps]) * m_lag[b]
            total = prod if total is None else total + prod
        acc = total[0:8, :]
        for i in range(1, taps // 8):
            acc = acc + pltpu.roll(total[8 * i : 8 * i + 8, :], taps - 8 * i, 1)
        for bit in (1, 2, 4):
            acc = jnp.where((sub & bit) != 0, pltpu.roll(acc, taps - bit, 1), acc)
        tacc[slot, g : g + 1, :] = jnp.sum(acc, axis=0, keepdims=True)

    def rows_sum(value):
        return jnp.sum(value.reshape(piece // 8, 8, LANES), axis=0)

    def finish_rows(t, slot, r0):
        cols = columns(t)
        span = slice(r0, r0 + piece)

        def gather(at, value):
            if r0:
                facc[at : at + 8, :] += value
            else:
                facc[at : at + 8, :] = value

        valid = iota((piece, LANES), 0) + r0 < filled
        skip = skip_ref[:, cols]
        mix = mix_ref[span, cols].astype(F32)
        mgr = mgr_ref[span, cols].astype(F32)
        gated = yacc[slot, span, :] + skip * mix
        back = bacc[slot, span, :] + skip * mgr
        gather(skips, rows_sum(mix * mgr))
        hyena_ref[span, cols] = jnp.where(
            valid, query_ref[span, cols].astype(F32) * gated, 0.0
        ).astype(BF)
        out_refs = (qb_ref, kb_ref, vb_ref)
        factors = (og_ref, values_ref, keys_ref)
        for w, (out_ref, ref, value) in enumerate(zip(out_refs, factors, (gated, back, back))):
            rounded = jnp.where(valid, ref[span, cols].astype(F32) * value, 0.0).astype(BF)
            out_ref[span, cols] = rounded
            grad = rounded.astype(F32)
            back_rows[w, PAD + r0 : PAD + r0 + piece, :] = grad
            if r0 == 0:
                head_ref[w * PAD : (w + 1) * PAD, cols] = grad[0:PAD].astype(BF)
            for j in range(short):
                source = ext[slot, w, 2 * PAD + r0 - j : 2 * PAD + r0 - j + piece, :]
                gather((w * short + j) * 8, rows_sum(source * grad))

    def finish_sums(t, slot):
        for k in range(docs):
            edge = scal[2 + k] - scal[0]

            @pl.when(jnp.logical_and(edge > -PAD, edge < rows))
            def _(k=k, edge=edge):
                size = scal[3 + k] - scal[2 + k] if k + 1 < docs else rows
                line = iota((PAD, LANES), 0)
                for w in range(3):
                    grad = back_rows[w, pl.ds(PAD + edge, PAD), :]
                    for j in range(1, short):
                        source = ext[slot, w, pl.ds(2 * PAD + edge - j, PAD), :]
                        drop = jnp.where(line < jnp.minimum(size, j), source * grad, 0.0)
                        at = (w * short + j) * 8
                        facc[at : at + 8, :] -= drop

        lines = sums_ref.shape[0] // count
        summed = jnp.sum(facc[...].reshape(lines - groups, 8, LANES), axis=1)
        packed = jnp.concatenate([summed, tacc[slot]], axis=0).astype(BF)
        sums_ref[pl.ds(pl.multiple_of(t * lines, lines), lines), :] = packed

    def tile(t, carry):
        slot = t % 2
        before = jnp.maximum(t - 1, 0)
        setup(t, slot)
        for g in range(groups):
            group(t, slot, g)
            finish_rows(before, 1 - slot, g * piece)
        finish_sums(before, 1 - slot)
        return carry

    lax.fori_loop(0, count, tile, 0)
    for g in range(groups):
        finish_rows(count - 1, (count - 1) % 2, g * piece)
    finish_sums(count - 1, (count - 1) % 2)


def unfeaturize_kernel(
    docs, short, firsts, facts, qb_ref, kb_ref, vb_ref, halo_ref, taps_ref, *rest
):
    outs = rest[-5:-2]
    dist, ext = rest[-2:]
    scal = Layout(firsts, facts)
    rows, width = qb_ref.shape
    filled = scal[1]

    @pl.when(pl.program_id(0) == 0)
    def _():
        fill_dist(scal, docs, dist)

    def tile(t, carry):
        cols = pl.ds(pl.multiple_of(t * LANES, LANES), LANES)
        taps_of = [taps_ref[w, :, cols].astype(F32) for w in range(3)]
        halo = halo_ref[:, cols].astype(F32)
        for w, ref in enumerate((qb_ref, kb_ref, vb_ref)):
            ext[w, 0:rows, :] = ref[:, cols].astype(F32)
            ext[w, pl.ds(filled, PAD), :] = halo[w * PAD : (w + 1) * PAD]
        for r0 in range(0, rows, STRIP):
            span = slice(r0, r0 + STRIP)

            def strip(masked, r0=r0, span=span):
                valid = iota((STRIP, LANES), 0) + r0 < filled
                for w in range(3):
                    acc = None
                    for j in range(short):
                        source = ext[w, r0 + j : r0 + j + STRIP, :]
                        term = taps_of[w][j : j + 1, :] * source
                        if masked and j:
                            term = jnp.where(dist[r0 + j : r0 + j + STRIP, :] >= j, term, 0.0)
                        acc = term if acc is None else acc + term
                    outs[w][span, cols] = jnp.where(valid, acc, 0.0).astype(BF)

            either(crosses(scal, docs, r0 - PAD, r0 + STRIP + PAD), strip)
        return carry

    lax.fori_loop(0, width // LANES, tile, 0)


def call(kernel, grid, ins, outs, scratch, args, scal, aliases=None, cost=None):
    specs = pltpu.PrefetchScalarGridSpec(
        num_scalar_prefetch=2, grid=grid, in_specs=[s for s in ins],
        out_specs=[s for s, _ in outs], scratch_shapes=scratch,
    )
    return pl.pallas_call(
        kernel, grid_spec=specs, out_shape=[o for _, o in outs],
        input_output_aliases=aliases or {},
        compiler_params=pltpu.CompilerParams(
            dimension_semantics=("arbitrary",), vmem_limit_bytes=56 * 1024 * 1024
        ),
        cost_estimate=cost,
    )(*scal, *args)


def shards(
    query_in, key_in, value_in, out_grad, fill_counts, doc_starts, feat_taps, mix_taps, skip_gain
):
    rows, channels = query_in.shape
    short = feat_taps.shape[1]
    groups, taps = mix_taps.shape
    docs = doc_starts.shape[0]
    per_group = channels // groups
    shard_count, mine = lax.axis_size("ctx"), lax.axis_index("ctx")
    filled = fill_counts[0]

    def tail_rows(source):
        return lax.dynamic_slice_in_dim(source, filled - PAD, PAD, 0)

    tails = jnp.concatenate([tail_rows(s) for s in (query_in, key_in, value_in)], axis=0)
    halo = shift(tails, "ctx", 1)
    later = jnp.arange(shard_count, dtype=jnp.int32) > mine
    firsts = lax.psum(jnp.where(later, filled, 0).astype(jnp.int32), "ctx")
    facts = jnp.concatenate([mine[None].astype(jnp.int32), fill_counts, doc_starts])
    scal = (firsts, facts)

    slots = 3 * short + 1
    slots = slots + (-slots) % 8
    hfwd = mix_taps.astype(F32)
    hrev = jnp.concatenate([hfwd[:, :1], hfwd[:, :0:-1]], axis=1)
    skip = skip_gain[None, :]

    tile_count = channels // LANES
    early = max(1, tile_count * EARLY // 8)
    sizes = [early * LANES, (tile_count - early) * LANES]
    starts = [0, early * LANES]
    wide = math.gcd(math.gcd(sizes[0], sizes[1]), WIDE)
    tiles = wide // LANES
    bf = lambda *shape: jax.ShapeDtypeStruct(shape, BF)

    def cols(height, offset=0):
        return pl.BlockSpec((height, wide), lambda i, *s: (0, i + offset))

    def taps_spec(offset):
        return pl.BlockSpec((3, short, wide), lambda i, *s: (0, 0, i + offset))

    featured, sent_mix, sent_grad = [], [], []
    for c, per_chunk in enumerate(sizes):
        off, steps = starts[c] // wide, per_chunk // wide
        full = cols(rows, off)
        outs = call(
            functools.partial(featurize_kernel, docs, short), (steps,),
            [full] * 4 + [cols(3 * PAD, off), taps_spec(off)],
            [(cols(rows), bf(rows, per_chunk))] * 5 + [(cols(taps), bf(taps, per_chunk))] * 2,
            [
                pltpu.VMEM((rows, LANES), jnp.int32),
                pltpu.VMEM((3, PAD + rows, LANES), F32),
                pltpu.VMEM((rows, LANES), F32),
            ],
            (query_in, key_in, value_in, out_grad, halo, feat_taps), scal,
            cost=pl.CostEstimate(flops=50 * rows * per_chunk, bytes_accessed=20 * rows * per_chunk, transcendentals=0),
        )
        featured.append(outs)
        sent_mix.append(shift(outs[5], "ctx", 1))
        sent_grad.append(shift(outs[6], "ctx", -1))

    hyena = sums = heads = None
    backs = []
    lines = slots + LANES // per_group
    blocks = rows // taps
    for c, per_chunk in enumerate(sizes):
        off, steps = starts[c] // wide, per_chunk // wide
        query, keys, values, mix, mgr = featured[c][:5]
        full = cols(rows, off)
        ins = [cols(taps), cols(rows), cols(rows), cols(taps)] + [cols(rows)] * 3 + [full] * 4
        ins += [cols(3 * PAD, off)]
        gspec = pl.BlockSpec((wide // per_group, taps), lambda i, *s, off=off: (i + off, 0))
        ins += [gspec, gspec, cols(1, off)]
        args = [sent_mix[c], mix, mgr, sent_grad[c], query, keys, values, out_grad]
        args += [query_in, key_in, value_in, halo, hfwd, hrev, skip]
        aliases = None
        if hyena is not None:
            ins += [pl.BlockSpec(memory_space=pl.ANY)] * 3
            args += [hyena, sums, heads]
            aliases = {len(args) - 1: 0, len(args): 1, len(args) + 1: 2}
        outs = call(
            functools.partial(mix_kernel, docs, short, per_group), (steps,), ins,
            [
                (full, bf(rows, channels)),
                (
                    pl.BlockSpec((tiles * lines, LANES), lambda i, *s, off=off: (i + off, 0)),
                    bf(channels // LANES * lines, LANES),
                ),
                (cols(3 * PAD, off), bf(3 * PAD, channels)),
            ]
            + [(cols(rows), bf(rows, per_chunk))] * 3,
            [
                pltpu.VMEM((blocks, taps, 2 * taps), BF),
                pltpu.VMEM((blocks, taps, 2 * taps), BF),
                pltpu.VMEM((blocks, taps, taps), F32),
                pltpu.VMEM((2, 3, 3 * PAD + rows, LANES), F32),
                pltpu.VMEM((rows + taps, LANES), BF),
                pltpu.VMEM((rows + taps, LANES), F32),
                pltpu.VMEM((rows + taps, LANES), BF),
                pltpu.VMEM((2, rows, LANES), F32),
                pltpu.VMEM((2, rows, LANES), F32),
                pltpu.VMEM((8 * slots, LANES), F32),
                pltpu.VMEM((3, rows + 2 * PAD, LANES), F32),
                pltpu.VMEM((2, LANES // per_group, LANES), F32),
            ],
            args, scal, aliases,
            cost=pl.CostEstimate(flops=2000 * rows * per_chunk, bytes_accessed=40 * rows * per_chunk, transcendentals=0),
        )
        hyena, sums, heads = outs[:3]
        backs.append(outs[3:6])

    next_heads = shift(heads, "ctx", -1)
    grads = None
    for c, per_chunk in enumerate(sizes):
        off, steps = starts[c] // wide, per_chunk // wide
        ins = [cols(rows)] * 3 + [cols(3 * PAD, off), taps_spec(off)]
        args = list(backs[c]) + [next_heads, feat_taps]
        aliases = None
        if grads is not None:
            for w in range(3):
                ins.append(pl.BlockSpec(memory_space=pl.ANY))
                args.append(grads[w])
            aliases = {len(args) - 1 + w: w for w in range(3)}
        grads = call(
            functools.partial(unfeaturize_kernel, docs, short), (steps,), ins,
            [(cols(rows, off), bf(rows, channels))] * 3,
            [
                pltpu.VMEM((rows + 2 * PAD, LANES), jnp.int32),
                pltpu.VMEM((3, rows + 2 * PAD, LANES), F32),
            ],
            args, scal, aliases,
            cost=pl.CostEstimate(flops=50 * rows * per_chunk, bytes_accessed=12 * rows * per_chunk, transcendentals=0),
        )

    height = sums.shape[0]
    extra = (-height) % shard_count
    payload = jnp.pad(sums, ((0, extra), (0, 0))) if extra else sums
    share = payload.shape[0] // shard_count
    pieces = lax.all_to_all(payload, "ctx", 0, 0, tiled=True)
    summed = jnp.sum(pieces.reshape(shard_count, share, LANES).astype(F32), axis=0).astype(BF)
    spread = jnp.broadcast_to(summed[None], (shard_count, share, LANES)).reshape(-1, LANES)
    whole = lax.all_to_all(spread, "ctx", 0, 0, tiled=True)[:height].astype(F32)
    total_params = (groups * taps + channels * (1 + 3 * short)) * lax.axis_size("tp")
    whole_sq = lax.psum(jnp.sum(whole * whole), "tp")
    factor = lax.rsqrt(whole_sq / total_params + 1e-06)
    scaled = (whole * factor).reshape(channels // LANES, lines, LANES)
    mix_part = scaled[:, slots:].reshape(groups, taps)
    mix_out = jnp.concatenate([mix_part[:, :1], mix_part[:, :0:-1]], axis=1)
    feat = scaled[:, : 3 * short + 1].transpose(1, 0, 2).reshape(3 * short + 1, channels)
    feat_out = feat[: 3 * short].reshape(3, short, channels)
    skip_out = feat[3 * short]
    return (hyena, grads[0], grads[1], grads[2], mix_out, skip_out, feat_out)


def solution(mesh):
    stream = P("ctx", "tp")
    in_specs = (
        stream, stream, stream, stream, P("ctx"), P(), P(None, None, "tp"), P("tp", None), P("tp"),
    )
    out_specs = (stream, stream, stream, stream, P("tp", None), P("tp"), P(None, None, "tp"))
    return jax.shard_map(
        shards, mesh=mesh, in_specs=in_specs, out_specs=out_specs,
        check_vma=False,
    )
```

time: 196 us -> 202 us (1.031); the launches traced: 198 us -> 201 us
  waiting for transfers between devices: 20.8 us -> 35.3 us
  Pallas kernels: 108 us -> 99.5 us
  other arithmetic: 8.27 us -> 4.29 us
  local copies, waits for them, and re-layouts: 11.8 us -> 8.04 us
  blocking collectives: 28.9 us -> 31.2 us
    psum x0 -> x1, blocking collectives: none -> 15.6 us  [shards(): firsts = lax.psum(jnp.where(later, filled, 0).astype(jnp.int32), 'ctx')]
    unnamed x1 -> x0, blocking collectives: 14.7 us -> none
    ppermute x7 -> x6, waiting for transfers between devices: 20.8 us -> 35.3 us  [shift(): return lax.ppermute(value, axis, pairs)]
    pallas_call x6, Pallas kernels: 108 us -> 99.5 us  [call(): pl.pallas_call(kernel, grid_spec=specs, out_shape=[o for _, o in outs], i...]
    unnamed x27 -> x14, local copies, waits for them, and re-layouts: 6.02 us -> 3.22 us
    ppermute x7 -> x6, starting transfers between devices: 14.9 us -> 16.6 us  [shift(): return lax.ppermute(value, axis, pairs)]
  transfers between devices with their start and end apart: 8 -> 7, of which waited for: 2 -> 3; matrix products, arithmetic and copies ran while one was open for 4% -> 1% of each run, Pallas kernels for 27% -> 20%
where the time goes in v2:
time: 202 us; the launch traced here: 201 us
  Pallas kernels  99.5 us (49%)
  waiting for transfers between devices  35.3 us (17%)
  blocking collectives  31.2 us (15%)
  starting transfers between devices  20.1 us (10%)
  local copies, waits for them, and re-layouts  8.04 us (4%)
  other arithmetic  4.29 us (2%)
  between operations  2.18 us (1%)
    pallas_call x6, Pallas kernels, call(): pl.pallas_call(kernel, grid_spec=specs, out_shape=[o for _, o in outs], i...  99.5 us
    ppermute x6, waiting for transfers between devices, shift(): return lax.ppermute(value, axis, pairs)  35.3 us
    ppermute x6, starting transfers between devices, shift(): return lax.ppermute(value, axis, pairs)  16.6 us
    psum x1, blocking collectives, shards(): firsts = lax.psum(jnp.where(later, filled, 0).astype(jnp.int32), 'ctx')  15.6 us
    all_to_all x1, blocking collectives, shards(): pieces = lax.all_to_all(payload, 'ctx', 0, 0, tiled=True)  12.5 us
  transfers between devices with their start and end apart: 7, of which 3 were waited for; matrix products, arithmetic and copies ran while one was open for 1% of the time, Pallas kernels for 20%

profile of v2, /device:TPU:0, one launch (start us, length us, event | category | flops | bytes accessed | tf_op | source)
XLA Modules:
  0.0 200.6 jit_solution(14254477991276995610)
XLA Ops:
  1.3 0.9 constant_dynamic-slice_fusion.2
  2.2 1.0 constant_dynamic-slice_fusion
  3.3 4.9 %collective-permute-start = (bf16[24,4096]{1,0:T(8,128)(2,1)S(1)}, bf16[24,4096]{1,0:T(8,128)(2,1)S(1)}, u32[]{:S(2)}, u32[]{:S(2)}) collective-permute-start(bf16[24,4096]{1,0:T(8,128)(2,1)S(1)} %pad_maximum_fusion), channel_id=1, source_target_pairs={{0,2},{2,4},{4,6},{6,8},{8,10},{10,12},{12,14},{14,16},{16,18},{18... | collective-permute-start | bytes 589832 | tf_op jit(solution)/shard_map/ppermute | solution.py:24
  8.2 15.6 %psum.14.firsts = s32[16]{0:T(128)} all-reduce(s32[16]{0:T(128)S(1)} %compare_select_fusion), channel_id=1, replica_groups=mesh['ctx'=16,'tp'=2] {'ctx'}, use_global_device_ids=true, to_apply=%region_0.1 | all-reduce | flops 16 | bytes 128 | tf_op jit(solution)/shard_map/psum | solution.py:362
  23.8 1.2 pad_add_fusion.facts
  25.1 0.7 copy-done
  25.8 11.3 %shard_map.144 = (bf16[256,2560]{1,0:T(8,128)(2,1)}, bf16[256,2560]{1,0:T(8,128)(2,1)}, bf16[256,2560]{1,0:T(8,128)(2,1)}, bf16[256,2560]{1,0:T(8,128)(2,1)}, bf...) custom-call(s32[16]{0:T(128)} %psum.14.firsts, s32[6]{0:T(128)} %pad_add_fusion.facts, ...), custom_call_target="tpu_custom_call" | custom-call | flops 32768000 | bytes 13107200 | tf_op jit(solution)/shard_map/pallas_call | solution.py:335
  37.1 3.5 %collective-permute-start.1 = (bf16[128,2560]{1,0:T(8,128)(2,1)}, bf16[128,2560]{1,0:T(8,128)(2,1)S(1)}, u32[]{:S(2)}, u32[]{:S(2)}) collective-permute-start(bf16[128,2560]{1,0:T(8,128)(2,1)} %get-tuple-element.39), channel_id=1, source_target_pairs={{0,2},{2,4},{4,6},{6,8},{8,10},{10,12},{12,14},{14,16},{16,18},{18... | collective-permute-start | bytes 1966088 | tf_op jit(solution)/shard_map/ppermute | solution.py:24
  40.6 1.4 collective-permute-start.2
  42.0 8.0 %shard_map.145 = (bf16[256,1536]{1,0:T(8,128)(2,1)}, bf16[256,1536]{1,0:T(8,128)(2,1)}, bf16[256,1536]{1,0:T(8,128)(2,1)}, bf16[256,1536]{1,0:T(8,128)(2,1)}, bf...) custom-call(s32[16]{0:T(128)} %psum.14.firsts, s32[6]{0:T(128)} %pad_add_fusion.facts, ...), custom_call_target="tpu_custom_call" | custom-call | flops 19660800 | bytes 7864320 | tf_op jit(solution)/shard_map/pallas_call | solution.py:335
  50.0 4.2 %collective-permute-start.3 = (bf16[128,1536]{1,0:T(8,128)(2,1)}, bf16[128,1536]{1,0:T(8,128)(2,1)S(1)}, u32[]{:S(2)}, u32[]{:S(2)}) collective-permute-start(bf16[128,1536]{1,0:T(8,128)(2,1)} %get-tuple-element.46), channel_id=1, source_target_pairs={{0,2},{2,4},{4,6},{6,8},{8,10},{10,12},{12,14},{14,16},{16,18},{18... | collective-permute-start | bytes 1179656 | tf_op jit(solution)/shard_map/ppermute | solution.py:24
  54.3 1.3 collective-permute-start.4
  55.6 0.7 convert_element_type.11.hfwd_ref
  56.5 0.8 pad_maximum_fusion.1.hrev_ref
  57.3 25.0 %collective-permute-done.3.prev_ref = bf16[128,1536]{1,0:T(8,128)(2,1)S(1)} collective-permute-done((bf16[128,1536]{1,0:T(8,128)(2,1)}, bf16[128,1536]{1,0:T(8,128)(2,1)S(1)}, u32[]{:S(2)}, u32[]{:S(2)}) %collective-permute-start.3) | collective-permute-done | bytes 393248 | tf_op jit(solution)/shard_map/ppermute | solution.py:24
  82.3 1.8 collective-permute-done.4.next_ref
  84.1 0.8 copy-done.6
  84.8 24.2 %shard_map.146 = (bf16[256,4096]{1,0:T(8,128)(2,1)}, bf16[1024,128]{1,0:T(8,128)(2,1)}, bf16[24,4096]{1,0:T(8,128)(2,1)}, bf16[256,1536]{1,0:T(8,128)(2,1)}, bf1...) custom-call(s32[16]{0:T(128)} %psum.14.firsts, s32[6]{0:T(128)} %pad_add_fusion.facts, bf16[128,1536]{1,0:T(8,128)(2,1)} %copy-done.5, ...), custom_call_target="tpu_custom_call" | custom-call | flops 786432000 | bytes 15728640 | tf_op jit(solution)/shard_map/pallas_call | solution.py:335
  109.1 0.8 copy-done.3
  110.2 38.1 %shard_map.147 = (bf16[256,4096]{1,0:T(8,128)(2,1)}, bf16[1024,128]{1,0:T(8,128)(2,1)}, bf16[24,4096]{1,0:T(8,128)(2,1)}, bf16[256,2560]{1,0:T(8,128)(2,1)}, bf1...) custom-call(s32[16]{0:T(128)} %psum.14.firsts, ...), custom_call_target="tpu_custom_call", output_to_operand_aliasing={{0}: (17, {}), {1}: (18, {}), {2}: (19, {})} | custom-call | flops 1310720000 | bytes 26214400 | tf_op jit(solution)/shard_map/pallas_call | solution.py:335
  148.3 12.5 %all_to_all.15 = bf16[16,64,128]{2,1,0:T(8,128)(2,1)S(1)} all-to-all(bf16[16,64,128]{2,1,0:T(8,128)(2,1)} %bitcast.19), channel_id=1, replica_groups=mesh['ctx'=16,'tp'=2] {'ctx'}, dimensions={0} | all-to-all | bytes 524288 | tf_op jit(solution)/shard_map/all_to_all | solution.py:483
  160.8 0.8 broadcast_in_dim.24
  161.5 3.5 %all-to-all-start.1 = ((bf16[16,64,128]{2,1,0:T(8,128)(2,1)}), bf16[16,64,128]{2,1,0:T(8,128)(2,1)S(1)}, u32[]{:S(2)}, u32[]{:S(2)}) async-start(bf16[16,64,128]{2,1,0:T(8,128)(2,1)} %broadcast_in_dim.24), calls=%async_computation.1 | async-start | bytes 524288 | tf_op jit(solution)/shard_map/all_to_all | solution.py:486
  165.1 1.3 collective-permute-start.5
  166.4 8.5 %collective-permute-done.5.halo_ref = bf16[24,4096]{1,0:T(8,128)(2,1)S(1)} collective-permute-done((bf16[24,4096]{1,0:T(8,128)(2,1)}, bf16[24,4096]{1,0:T(8,128)(2,1)S(1)}, u32[]{:S(2)}, u32[]{:S(2)}) %collective-permute-start.5) | collective-permute-done | bytes 196640 | tf_op jit(solution)/shard_map/ppermute | solution.py:24
  174.9 0.7 copy-done.2
  175.6 7.3 %shard_map.148 = (bf16[256,4096]{1,0:T(8,128)(2,1)}, bf16[256,4096]{1,0:T(8,128)(2,1)}, bf16[256,4096]{1,0:T(8,128)(2,1)}) custom-call(s32[16]{0:T(128)} %psum.14.firsts, s32[6]{0:T(128)} %pad_add_fusion.facts, bf16[256,1536]{1,0:T(8,128)(2,1)} %get-tuple-element.61.qb_ref, bf16[256,1536]{1,0:T(8,128)(2,1)} %get-tuple-element.62.kb_ref, ...), custom_call_target="tpu_custom_call" | custom-call | flops 19660800 | bytes 4718592 | tf_op jit(solution)/shard_map/pallas_call | solution.py:335
  182.9 0.7 fusion
  183.7 10.5 %shard_map.149 = (bf16[256,4096]{1,0:T(8,128)(2,1)}, bf16[256,4096]{1,0:T(8,128)(2,1)}, bf16[256,4096]{1,0:T(8,128)(2,1)}) custom-call(s32[16]{0:T(128)} %psum.14.firsts, s32[6]{0:T(128)} %pad_add_fusion.facts, bf16[256,2560]{1,0:T(8,128)(2,1)} %get-tuple-element.57.qb_ref, ...), custom_call_target="tpu_custom_call", output_to_operand_aliasing={{0}: (7, {}), {1}: (8, {}), {2}: (9, {})} | custom-call | flops 32768000 | bytes 7864320 | tf_op jit(solution)/shard_map/pallas_call | solution.py:335
  194.1 3.1 %psum.15 = f32[]{:T(128)} all-reduce(f32[]{:T(128)} %fusion), channel_id=1, replica_groups=mesh['ctx'=16,'tp'=2] {'tp'}, use_global_device_ids=true, to_apply=%region_3.4 | all-reduce | flops 1 | bytes 8 | tf_op jit(solution)/shard_map/psum | solution.py:488
  199.0 0.8 reshape.40
  199.8 0.8 pad_maximum_fusion.2
  (27 shorter events, 1.7 us)
Async XLA Ops:
  3.3 21.8 %collective-permute-start = (bf16[24,4096]{1,0:T(8,128)(2,1)S(1)}, bf16[24,4096]{1,0:T(8,128)(2,1)S(1)}, u32[]{:S(2)}, u32[]{:S(2)}) collective-permute-start(bf16[24,4096]{1,0:T(8,128)(2,1)S(1)} %pad_maximum_fusion), channel_id=1, source_target_pairs={{0,2},{2,4},{4,6},{6,8},{8,10},{10,12},{12,14},{14,16},{16,18},{18... | collective-permute-start | bytes 589832 | tf_op jit(solution)/shard_map/ppermute | solution.py:24
  25.1 0.7 copy-start
  37.1 72.0 %collective-permute-start.1 = (bf16[128,2560]{1,0:T(8,128)(2,1)}, bf16[128,2560]{1,0:T(8,128)(2,1)S(1)}, u32[]{:S(2)}, u32[]{:S(2)}) collective-permute-start(bf16[128,2560]{1,0:T(8,128)(2,1)} %get-tuple-element.39), channel_id=1, source_target_pairs={{0,2},{2,4},{4,6},{6,8},{8,10},{10,12},{12,14},{14,16},{16,18},{18... | collective-permute-start | bytes 1966088 | tf_op jit(solution)/shard_map/ppermute | solution.py:24
  40.6 15.0 %copy-start.1 = (bf16[256,128]{1,0:T(8,128)(2,1)S(1)}, bf16[256,128]{1,0:T(8,128)(2,1)}, u32[]{:S(2)}) copy-start(bf16[256,128]{1,0:T(8,128)(2,1)} %param.16) | copy-start | bytes 196612
  40.6 68.5 %collective-permute-start.2 = (bf16[128,2560]{1,0:T(8,128)(2,1)}, bf16[128,2560]{1,0:T(8,128)(2,1)S(1)}, u32[]{:S(2)}, u32[]{:S(2)}) collective-permute-start(bf16[128,2560]{1,0:T(8,128)(2,1)} %get-tuple-element.42), channel_id=1, source_target_pairs={{2,0},{4,2},{6,4},{8,6},{10,8},{12,10},{14,12},{16,14},{18,16},{20... | collective-permute-start | bytes 1966088 | tf_op jit(solution)/shard_map/ppermute | solution.py:24
  50.0 32.2 %collective-permute-start.3 = (bf16[128,1536]{1,0:T(8,128)(2,1)}, bf16[128,1536]{1,0:T(8,128)(2,1)S(1)}, u32[]{:S(2)}, u32[]{:S(2)}) collective-permute-start(bf16[128,1536]{1,0:T(8,128)(2,1)} %get-tuple-element.46), channel_id=1, source_target_pairs={{0,2},{2,4},{4,6},{6,8},{8,10},{10,12},{12,14},{14,16},{16,18},{18... | collective-permute-start | bytes 1179656 | tf_op jit(solution)/shard_map/ppermute | solution.py:24
  54.3 29.8 %collective-permute-start.4 = (bf16[128,1536]{1,0:T(8,128)(2,1)}, bf16[128,1536]{1,0:T(8,128)(2,1)S(1)}, u32[]{:S(2)}, u32[]{:S(2)}) collective-permute-start(bf16[128,1536]{1,0:T(8,128)(2,1)} %get-tuple-element.49), channel_id=1, source_target_pairs={{2,0},{4,2},{6,4},{8,6},{10,8},{12,10},{14,12},{16,14},{18,16},{20... | collective-permute-start | bytes 1179656 | tf_op jit(solution)/shard_map/ppermute | solution.py:24
  82.3 1.8 copy-start.5
  84.1 0.8 copy-start.6
  109.1 0.9 copy-start.3
  109.1 1.1 copy-start.4
  161.5 21.4 %all-to-all-start.1 = ((bf16[16,64,128]{2,1,0:T(8,128)(2,1)}), bf16[16,64,128]{2,1,0:T(8,128)(2,1)S(1)}, u32[]{:S(2)}, u32[]{:S(2)}) async-start(bf16[16,64,128]{2,1,0:T(8,128)(2,1)} %broadcast_in_dim.24), calls=%async_computation.1 | async-start | bytes 524288 | tf_op jit(solution)/shard_map/all_to_all | solution.py:486
  165.1 9.8 %collective-permute-start.5 = (bf16[24,4096]{1,0:T(8,128)(2,1)}, bf16[24,4096]{1,0:T(8,128)(2,1)S(1)}, u32[]{:S(2)}, u32[]{:S(2)}) collective-permute-start(bf16[24,4096]{1,0:T(8,128)(2,1)} %get-tuple-element.60), channel_id=1, source_target_pairs={{2,0},{4,2},{6,4},{8,6},{10,8},{12,10},{14,12},{16,14},{18,16},{20... | collective-permute-start | bytes 589832 | tf_op jit(solution)/shard_map/ppermute | solution.py:24
  174.9 0.7 copy-start.2
